TPU v7x, 32 devices: a whole 2x2x4 slice. The times are simulated.
32 devices in a mesh: frame: 8 (over z, x), row: 4 (over y, core).
Axes of the slice: x: 2, y: 2, z: 4, core: 2. Of those that a mesh axis runs over, the one named last changes fastest.
Arguments:
- frames: float32 [64, 128, 2048], P('frame', 'row'), may hold values from -12 to 12
Outputs:
- estimate: float32 [128, 2048], P('row')
All inputs are finite; a program needn't handle non-finite values.
Results may differ from a plain program's by a relative error of at most 0.00002.
Values sent between devices are 32-bit elements; how exact they have to be, the bound alone decides.
No kernel may reach another device: no remote copies, remote signals or barrier semaphores. Data moves between devices by JAX's collectives and lax.ppermute only.
A program may use at most 64 MiB of HBM per device.

v0:
```python
import jax
import jax.numpy as jnp
from jax import lax
from jax.sharding import PartitionSpec as P

FRAMES = 64
ROUNDS = 3


GUIDE_EPS = 0.05
CAUCHY_SCALE = 0.5


def with_halo(x, sides, width):
    for axis, dim in sides:
        count, length = (lax.axis_size(axis), x.shape[dim])
        up = [(i, (i + 1) % count) for i in range(count - 1)]
        down = [(j, i) for i, j in up]
        last = lax.slice_in_dim(x, length - width, length, axis=dim)
        initial = lax.slice_in_dim(x, 0, width, axis=dim)
        before = lax.ppermute(last, axis, up)
        after = lax.ppermute(initial, axis, down)
        x = jnp.concatenate([before, x, after], axis=dim)
    return x


def row_sum(field):
    length = field.shape[-2] - 8
    total = field[..., 0:length, :]
    for offset in range(1, 9):
        total = total + field[..., offset : offset + length, :]
    return total


def col_sum(field):
    width = field.shape[-1]
    padded = jnp.pad(field, [(0, 0)] * (field.ndim - 1) + [(4, 4)])
    total = padded[..., 0:width]
    for offset in range(1, 9):
        total = total + padded[..., offset : offset + width]
    return total


def window_count(first, length, limit):
    place = first + jnp.arange(length, dtype=jnp.int32)
    lower = jnp.maximum(place - 4, 0)
    upper = jnp.minimum(place + 4, limit - 1)
    return jnp.maximum(upper - lower + 1, 1).astype(jnp.float32)


def smooth(padded_rows, area):
    return col_sum(row_sum(padded_rows)) / area


def shards(frames):
    local_rows = frames.shape[1]
    width = frames.shape[2]
    height = local_rows * lax.axis_size("row")
    start = lax.axis_index("row") * local_rows
    col_counts = window_count(0, width, width)
    estimate = lax.psum(jnp.sum(frames, axis=0), "frame") / FRAMES
    depth = 4
    padded_frames = with_halo(frames, (("row", 1),), 4)
    stat_rows = local_rows + 2 * depth - 8
    stat_first = start - depth + 4
    stat_area = window_count(stat_first, stat_rows, height)[:, None] * col_counts[None, :]
    out_area = window_count(start, local_rows, height)[:, None] * col_counts[None, :]
    for round_index in range(ROUNDS):
        padded_guide = with_halo(estimate, (("row", 0),), 4)
        mean_guide = smooth(padded_guide, stat_area)
        variance = smooth(padded_guide * padded_guide, stat_area) - mean_guide * mean_guide
        mean_frame = smooth(padded_frames, stat_area)
        cross = smooth(padded_guide[None] * padded_frames, stat_area)
        slope = (cross - mean_guide * mean_frame) / (variance + GUIDE_EPS)
        offset_term = mean_frame - slope * mean_guide
        stacked = with_halo(jnp.stack((slope, offset_term)), (("row", 2),), 4)
        slope_rows = stacked[0]
        offset_rows = stacked[1]
        filtered = smooth(slope_rows, out_area) * estimate[None] + smooth(offset_rows, out_area)
        gap = (filtered - estimate[None]) / CAUCHY_SCALE
        weight = 1.0 / (1.0 + gap * gap)
        weighted = jnp.sum(weight * frames, axis=0)
        total = jnp.sum(weight, axis=0)
        sums = lax.psum((weighted, total), "frame")
        estimate = sums[0] / sums[1]
    return estimate


def solution(mesh):
    return jax.shard_map(
        shards,
        mesh=mesh,
        in_specs=(P("frame", "row", None),),
        out_specs=P("row", None),
        check_vma=False,
    )
```

profile of v0, /device:TPU:0, one launch (start us, length us, event | category | flops | bytes accessed | tf_op | source)
XLA Modules:
  0.0 464.8 jit_solution(2341321879455873204)
XLA Ops:
  7.8 2.4 collective-permute-start.2
  11.7 1.8 constant_dynamic-update-slice_fusion.1
  13.5 2.4 collective-permute-done.3
  16.0 3.6 fusion.7
  19.7 75.9 %all-reduce.24.cloned.1.call-done = f32[32,2048]{1,0:T(8,128)} async-done(((f32[32,2048]{1,0:T(8,128)}), f32[32,2048]{1,0:T(8,128)}) %all-reduce.24.cloned.1.call-update) | async-done | bytes 262160 | tf_op jit(solution)/shard_map/psum | solution.py:61
  99.2 3.5 collective-permute-done.1
  103.2 2.5 slice_add_fusion.64
  106.1 1.9 fusion.74
  108.0 14.9 %subtract_bitcast_fusion.2 = (f32[1,8,32,2048]{3,2,1,0:T(8,128)S(1)}, f32[8,32,2048]{2,1,0:T(8,128)S(1)}, f32[8,32,2048]{2,1,0:T(8,128)}) fusion(f32[32,2048]{1,0:T(8,128)} %get-tuple-element.29, f32[32,2048]{1,0:T(8,128)S(1)} %get-tuple-element.28, f32[32,2048]{1,0:T(8,128)S(1)} %get-tuple-element.58, f32[8,32,2048]{2,1,0:T(8,128)} %slice_add_fusion.64, ...), kind=kLoop, calls=%fused_computation.150 | loop fusion | flops 12058624 | bytes 11272192 | tf_op jit(solution)/shard_map/stack | solution.py:76
  123.1 4.6 collective-permute-start.4
  129.2 2.3 collective-permute-done.5
  132.9 1.5 slice_add_fusion.56
  136.1 9.7 %fusion.102 = (f32[32,2048]{1,0:T(8,128)}, f32[32,2048]{1,0:T(8,128)}) fusion(f32[8,32,2048]{2,1,0:T(8,128)S(1)} %copy-done, f32[8,32,2048]{2,1,0:T(8,128)S(1)} %slice_add_fusion.48, f32[32,2048]{1,0:T(8,128)S(1)} %broadcast_multiply_fusion.4, f32[32,2048]{1,0:T(8,128)S(1)} %get-tuple-element.58, f32[8,32,2048]{2,1,0:T(8,128)S(1)} %slice_add_fusion.56), kind=kLoop, calls=%fused_computation.343 | loop fusion | flops 14548992 | bytes 7340032 | tf_op jit(solution)/shard_map/reduce_sum | solution.py:83
  145.8 77.5 %all-reduce.30.cloned.1.call-done = (f32[32,2048]{1,0:T(8,128)}, f32[32,2048]{1,0:T(8,128)}) async-done(((f32[32,2048]{1,0:T(8,128)}, f32[32,2048]{1,0:T(8,128)}), (f32[32,2048]{1,0:T(8,128)}, f32[32,2048]{1,0:T(8,128)})) %all-reduce.30.cloned.1.call-update) | async-done | bytes 524304 | tf_op jit(solution)/shard_map/psum | solution.py:84
  227.3 3.3 collective-permute-done.7
  231.3 1.5 slice_add_fusion.40
  234.3 4.5 subtract_bitcast_fusion.1
  239.0 4.6 collective-permute-start.8
  243.6 1.5 collective-permute-start.9
  245.2 2.2 collective-permute-done.9
  252.3 9.7 %fusion.101 = (f32[32,2048]{1,0:T(8,128)}, f32[32,2048]{1,0:T(8,128)}) fusion(f32[8,32,2048]{2,1,0:T(8,128)S(1)} %copy-done, f32[8,32,2048]{2,1,0:T(8,128)S(1)} %slice_add_fusion.24, f32[32,2048]{1,0:T(8,128)S(1)} %div.158, f32[32,2048]{1,0:T(8,128)S(1)} %get-tuple-element.58, f32[8,32,2048]{2,1,0:T(8,128)S(1)} %slice_add_fusion.32), kind=kLoop, calls=%fused_computation.342 | loop fusion | flops 14548992 | bytes 7340032 | tf_op jit(solution)/shard_map/reduce_sum | solution.py:83
  262.1 77.6 %all-reduce.28.cloned.1.call-done = (f32[32,2048]{1,0:T(8,128)}, f32[32,2048]{1,0:T(8,128)}) async-done(((f32[32,2048]{1,0:T(8,128)}, f32[32,2048]{1,0:T(8,128)}), (f32[32,2048]{1,0:T(8,128)}, f32[32,2048]{1,0:T(8,128)})) %all-reduce.28.cloned.1.call-update) | async-done | bytes 524304 | tf_op jit(solution)/shard_map/psum | solution.py:84
  342.1 1.6 collective-permute-start.11
  343.7 3.2 collective-permute-done.11
  347.6 1.5 slice_add_fusion.16
  350.6 4.5 subtract_bitcast_fusion
  355.3 4.6 collective-permute-start.12
  359.9 1.6 collective-permute-start.13
  361.5 2.2 collective-permute-done.13
  368.6 9.7 %fusion.100 = (f32[32,2048]{1,0:T(8,128)}, f32[32,2048]{1,0:T(8,128)}) fusion(f32[8,32,2048]{2,1,0:T(8,128)S(1)} %copy-done, f32[8,32,2048]{2,1,0:T(8,128)S(1)} %slice_add_fusion, f32[32,2048]{1,0:T(8,128)S(1)} %div.168, f32[32,2048]{1,0:T(8,128)S(1)} %get-tuple-element.58, f32[8,32,2048]{2,1,0:T(8,128)S(1)} %slice_add_fusion.8), kind=kLoop, calls=%fused_computation.341 | loop fusion | flops 14548992 | bytes 7340032 | tf_op jit(solution)/shard_map/reduce_sum | solution.py:83
  378.3 77.7 %all-reduce.26.cloned.1.call-done = (f32[32,2048]{1,0:T(8,128)}, f32[32,2048]{1,0:T(8,128)}) async-done(((f32[32,2048]{1,0:T(8,128)}, f32[32,2048]{1,0:T(8,128)}), (f32[32,2048]{1,0:T(8,128)}, f32[32,2048]{1,0:T(8,128)})) %all-reduce.26.cloned.1.call-update) | async-done | bytes 524304 | tf_op jit(solution)/shard_map/psum | solution.py:84
  456.0 1.8 div.178
  (67 shorter events, 32.8 us)
Async XLA Ops:
  6.5 89.1 %all-reduce.24.cloned.1.call-start = ((), (), s32[]{:S(2)}) async-start(), calls=%async_computation | async-start | bytes 524288 | tf_op jit(solution)/shard_map/psum | solution.py:61
  7.8 8.2 %collective-permute-start.2 = (f32[8,4,2048]{2,1,0:T(4,128)S(1)}, f32[8,4,2048]{2,1,0:T(4,128)S(1)}, u32[]{:S(2)}, u32[]{:S(2)}) collective-permute-start(f32[8,4,2048]{2,1,0:T(4,128)S(1)} %get-tuple-element.44), channel_id=1, source_target_pairs={{0,1},{1,2},{2,3},{4,5},{5,6},{6,7},{8,9},{9,10},{10,11},{12,13},{... | collective-permute-start | bytes 786440 | tf_op jit(solution)/shard_map/ppermute | solution.py:21
  10.3 5.8 %copy-start = (f32[8,32,2048]{2,1,0:T(8,128)S(1)}, f32[8,32,2048]{2,1,0:T(8,128)}, u32[]{:S(2)}) copy-start(f32[8,32,2048]{2,1,0:T(8,128)} %param.1) | copy-start | bytes 6291460
  10.3 5.7 %collective-permute-start.3 = (f32[8,4,2048]{2,1,0:T(4,128)S(1)}, f32[8,4,2048]{2,1,0:T(4,128)S(1)}, u32[]{:S(2)}, u32[]{:S(2)}) collective-permute-start(f32[8,4,2048]{2,1,0:T(4,128)S(1)} %get-tuple-element.45), channel_id=1, source_target_pairs={{1,0},{2,1},{3,2},{5,4},{6,5},{7,6},{9,8},{10,9},{11,10},{13,12},{... | collective-permute-start | bytes 786440 | tf_op jit(solution)/shard_map/ppermute | solution.py:22
  19.7 203.7 %all-reduce.30.cloned.1.call-start = ((), (), s32[]{:S(2)}) async-start(), calls=%async_computation.3 | async-start | bytes 1048576 | tf_op jit(solution)/shard_map/psum | solution.py:84
  96.6 2.6 collective-permute-start
  97.9 4.8 %collective-permute-start.1 = (f32[4,2048]{1,0:T(4,128)S(1)}, f32[4,2048]{1,0:T(4,128)S(1)}, u32[]{:S(2)}, u32[]{:S(2)}) collective-permute-start(f32[4,2048]{1,0:T(4,128)S(1)} %get-tuple-element.57), channel_id=1, source_target_pairs={{1,0},{2,1},{3,2},{5,4},{6,5},{7,6},{9,8},{10,9},{11,10},{13,12},{... | collective-permute-start | bytes 98312 | tf_op jit(solution)/shard_map/ppermute | solution.py:22
  105.7 2.3 copy-start.3
  123.1 6.1 %collective-permute-start.4 = (f32[2,8,4,2048]{3,2,1,0:T(4,128)S(1)}, f32[2,8,4,2048]{3,2,1,0:T(4,128)S(1)}, u32[]{:S(2)}, u32[]{:S(2)}) collective-permute-start(f32[2,8,4,2048]{3,2,1,0:T(4,128)S(1)} %get-tuple-element.40), channel_id=1, source_target_pairs={{0,1},{1,2},{2,3},{4,5},{5,6},{6,7},{8,9},{9,10},{10,11},{12,13},{... | collective-permute-start | bytes 1572872 | tf_op jit(solution)/shard_map/ppermute | solution.py:21
  127.7 3.8 collective-permute-start.5
  145.8 193.9 %all-reduce.28.cloned.1.call-start = ((), (), s32[]{:S(2)}) async-start(), calls=%async_computation.2 | async-start | bytes 1048576 | tf_op jit(solution)/shard_map/psum | solution.py:84
  224.5 2.8 collective-permute-start.6
  225.8 4.8 %collective-permute-start.7 = (f32[4,2048]{1,0:T(4,128)S(1)}, f32[4,2048]{1,0:T(4,128)S(1)}, u32[]{:S(2)}, u32[]{:S(2)}) collective-permute-start(f32[4,2048]{1,0:T(4,128)S(1)} %get-tuple-element.55), channel_id=1, source_target_pairs={{1,0},{2,1},{3,2},{5,4},{6,5},{7,6},{9,8},{10,9},{11,10},{13,12},{... | collective-permute-start | bytes 98312 | tf_op jit(solution)/shard_map/ppermute | solution.py:22
  231.3 3.0 copy-start.1
  239.0 6.1 %collective-permute-start.8 = (f32[2,8,4,2048]{3,2,1,0:T(4,128)S(1)}, f32[2,8,4,2048]{3,2,1,0:T(4,128)S(1)}, u32[]{:S(2)}, u32[]{:S(2)}) collective-permute-start(f32[2,8,4,2048]{3,2,1,0:T(4,128)S(1)} %get-tuple-element.38), channel_id=1, source_target_pairs={{0,1},{1,2},{2,3},{4,5},{5,6},{6,7},{8,9},{9,10},{10,11},{12,13},{... | collective-permute-start | bytes 1572872 | tf_op jit(solution)/shard_map/ppermute | solution.py:21
  243.6 3.8 collective-permute-start.9
  262.0 193.9 %all-reduce.26.cloned.1.call-start = ((), (), s32[]{:S(2)}) async-start(), calls=%async_computation.1 | async-start | bytes 1048576 | tf_op jit(solution)/shard_map/psum | solution.py:84
  340.8 2.9 collective-permute-start.10
  342.1 4.8 %collective-permute-start.11 = (f32[4,2048]{1,0:T(4,128)S(1)}, f32[4,2048]{1,0:T(4,128)S(1)}, u32[]{:S(2)}, u32[]{:S(2)}) collective-permute-start(f32[4,2048]{1,0:T(4,128)S(1)} %get-tuple-element.53), channel_id=1, source_target_pairs={{1,0},{2,1},{3,2},{5,4},{6,5},{7,6},{9,8},{10,9},{11,10},{13,12},{... | collective-permute-start | bytes 98312 | tf_op jit(solution)/shard_map/ppermute | solution.py:22
  347.6 3.0 copy-start.2
  355.3 6.2 %collective-permute-start.12 = (f32[2,8,4,2048]{3,2,1,0:T(4,128)S(1)}, f32[2,8,4,2048]{3,2,1,0:T(4,128)S(1)}, u32[]{:S(2)}, u32[]{:S(2)}) collective-permute-start(f32[2,8,4,2048]{3,2,1,0:T(4,128)S(1)} %get-tuple-element.36), channel_id=1, source_target_pairs={{0,1},{1,2},{2,3},{4,5},{5,6},{6,7},{8,9},{9,10},{10,11},{12,13},{... | collective-permute-start | bytes 1572872 | tf_op jit(solution)/shard_map/ppermute | solution.py:21
  359.9 3.8 collective-permute-start.13
Sparse Core Ops, SparseCore 0:
  19.8 75.7 all-reduce.23
  145.9 77.4 all-reduce.29
  262.2 77.4 all-reduce.27
  378.4 77.4 all-reduce.25
where the time goes:
time: 472 us; the launch traced here: 465 us
  waiting for transfers between devices  328 us (69%)
  other arithmetic  87.1 us (18%)
  starting transfers between devices  30.6 us (6%)
  between operations  14.2 us (3%)
  local copies, waits for them, and re-layouts  5.12 us (1%)
    psum x3, waiting for transfers between devices, shards(): sums = lax.psum((weighted, total), 'frame')  233 us
    psum x1, waiting for transfers between devices, shards(): estimate = lax.psum(jnp.sum(frames, axis=0), 'frame') / FRAMES  75.9 us
    reduce_sum x3, other arithmetic, shards(): total = jnp.sum(weight, axis=0)  29.1 us
    another operation x3, other arithmetic, shards(): stacked = with_halo(jnp.stack((slope, offset_term)), (('row', 2),), 4)  23.9 us
    ppermute x7, starting transfers between devices, with_halo(): before = lax.ppermute(last, axis, up)  20 us
    add x15, other arithmetic, row_sum(): total = total + field[..., offset:offset + length, :]  19.8 us
    ppermute x7, waiting for transfers between devices, with_halo(): after = lax.ppermute(initial, axis, down)  19.1 us
    ppermute x7, starting transfers between devices, with_halo(): after = lax.ppermute(initial, axis, down)  10.4 us
  transfers between devices with their start and end apart: 18, of which 11 were waited for; matrix products, arithmetic and copies ran while one was open for 0% of the time, Pallas kernels for 0%

commit v1 on v0

v1 whole, which is shorter than its diff:
```python
import functools

import jax
import jax.numpy as jnp
from jax import lax
from jax.experimental import pallas as pl
from jax.experimental.pallas import tpu as pltpu
from jax.sharding import PartitionSpec as P

ROUNDS = 3
RADIUS = 4
GUIDE_EPS = 0.05
CAUCHY_SCALE = 0.5

LANES = 128
GROUP = 8
BLOCK = 8
BOTH = ("frame", "row")


def lane_ids(shape):
    return lax.broadcasted_iota(jnp.int32, shape, len(shape) - 1)


def roll(x, shift):
    return pltpu.roll(x, shift % LANES, x.ndim - 1)


def col_box(v):
    s3 = v + roll(v, 1) + roll(v, -1)
    return s3 + roll(s3, 3) + roll(s3, -3)


def row_box(v):
    n = v.shape[0]
    s3 = v[0 : n - 2] + v[1 : n - 1] + v[2:n]
    return s3[0 : n - 8] + s3[3 : n - 5] + s3[6 : n - 2]


def count(place, limit):
    lower = jnp.maximum(place - RADIUS, 0)
    upper = jnp.minimum(place + RADIUS, limit - 1)
    return jnp.maximum(upper - lower + 1, 1).astype(jnp.float32)


def inverse_counts(first_row, rows, height, first_col, width):
    shape = (rows, GROUP, LANES)
    row = first_row + lax.broadcasted_iota(jnp.int32, shape, 0)
    col = first_col + lax.broadcasted_iota(jnp.int32, shape, 2)
    inside = jnp.logical_and(col >= 0, col < width)
    return jnp.where(inside, 1.0 / (count(row, height) * count(col, width)), 0.0)


def clear_edges(ref):
    zero = jnp.zeros((RADIUS, GROUP, LANES), jnp.float32)
    ref[0:RADIUS] = zero
    ref[ref.shape[0] - RADIUS :] = zero


def loop(total, step, body):
    def go(i, carry):
        body(pl.multiple_of(i * step, step))
        return carry

    lax.fori_loop(0, total // step, go, 0)


def pack_kernel(rows, x_ref, out_ref):
    half = rows // 2
    low = lane_ids((GROUP, LANES)) < LANES // 2
    for i in range(half):
        a = x_ref[pl.ds(i, GROUP, stride=rows), :]
        b = x_ref[pl.ds(i + half, GROUP, stride=rows), :]
        out_ref[0, i] = jnp.where(low, a, roll(b, 64))
        out_ref[1, i] = jnp.where(low, roll(a, 64), b)


def unpack_kernel(rows, r_ref, s_ref, left_ref, right_ref):
    n_row, half = r_ref.shape[0], rows // 2
    lane = lane_ids((GROUP, LANES))
    middle = jnp.logical_and(lane >= 32, lane < 96)
    slot = lane // 8

    def row_of(i):
        r, k = divmod(i, rows)
        v = r_ref[r, k % half]
        return v, k < half

    height = n_row * rows
    for p in range(height // 16):
        left = jnp.zeros((GROUP, LANES), jnp.float32)
        right = left
        for j in range(16):
            v, low = row_of(p * 16 + j)
            s_ref[p * 16 + j] = jnp.where(middle, roll(v, 32 if low else -32), 0.0)
            first = 0 if low else 64
            here = slot == j
            left = jnp.where(here, roll(v, 8 * j - first), left)
            right = jnp.where(here, roll(v, 8 * j - first - 56), right)
        left_ref[p] = left
        right_ref[p] = right


def stats_kernel(width, strip, s_ref, before_ref, after_ref, full_ref, mean_ref, est_ref, tmp, acc):
    g = pl.program_id(0)
    frames = pl.num_programs(0) * GROUP
    height = s_ref.shape[0]
    first_col = strip() * 64 - 32
    lane = lane_ids((GROUP, LANES))
    on_left = jnp.logical_and(lane >= 24, lane < 32)
    on_right = jnp.logical_and(lane >= 96, lane < 104)

    @pl.when(g == 0)
    def _():
        clear_edges(tmp)
        acc[...] = jnp.zeros_like(acc)

    def merge(i0):
        p = i0 // 16
        before, after = before_ref[p], after_ref[p]
        rows = []
        for j in range(16):
            v = s_ref[i0 + j]
            v = jnp.where(on_left, roll(before, 24 - 8 * j), v)
            v = jnp.where(on_right, roll(after, 96 - 8 * j), v)
            rows.append(v)
        v = jnp.stack(rows)
        full_ref[pl.ds(i0, 16)] = v
        acc[pl.ds(i0, 16)] += v
        tmp[pl.ds(i0 + RADIUS, 16)] = col_box(v)

    loop(height, 16, merge)

    def means(i0):
        ic = inverse_counts(i0, BLOCK, height, first_col, width)
        mean_ref[pl.ds(i0, BLOCK)] = row_box(tmp[pl.ds(i0, BLOCK + 8)]) * ic

    loop(height, BLOCK, means)

    @pl.when(g == pl.num_programs(0) - 1)
    def _():
        def finish(i0):
            est_ref[pl.ds(i0, BLOCK)] = jnp.sum(acc[pl.ds(i0, BLOCK)], axis=1) / frames

        loop(height, BLOCK, finish)


def round_kernel(
    width, strip, exchanged, last, n_frame, n_row,
    e_ref, before_ref, after_ref, s_ref, mean_ref, out_ref,
    est, guide, gain, mgain, scaled_e, scaled, twice, t1, t2, t3, acc_w, acc_t, flat,
):
    g = pl.program_id(0)
    height = s_ref.shape[0]
    first_col = strip() * 64 - 32

    @pl.when(g == 0)
    def _():
        clear_edges(t1)
        clear_edges(t2)
        clear_edges(t3)
        acc_w[...] = jnp.zeros_like(acc_w)
        acc_t[...] = jnp.zeros_like(acc_t)

        def spread(i0):
            e = e_ref[pl.ds(i0, BLOCK), :]
            if exchanged:
                lane = lane_ids(e.shape)
                e = jnp.where(lane < 32, roll(before_ref[pl.ds(i0, BLOCK), :], 64), e)
                e = jnp.where(lane >= 96, roll(after_ref[pl.ds(i0, BLOCK), :], 64), e)
            e = jnp.broadcast_to(e[:, None, :], (BLOCK, GROUP, LANES))
            est[pl.ds(i0, BLOCK)] = e
            t2[pl.ds(i0 + RADIUS, BLOCK)] = col_box(e)
            t3[pl.ds(i0 + RADIUS, BLOCK)] = col_box(e * e)

        loop(height, BLOCK, spread)

        def prepare(i0):
            here = pl.ds(i0, BLOCK)
            ic = inverse_counts(i0, BLOCK, height, first_col, width)
            m = row_box(t2[pl.ds(i0, BLOCK + 8)]) * ic
            var = row_box(t3[pl.ds(i0, BLOCK + 8)]) * ic - m * m
            inv = 1.0 / (var + GUIDE_EPS)
            e = est[here]
            guide[here] = m
            gain[here] = ic * inv
            mgain[here] = m * inv
            ic2 = ic * (1.0 / CAUCHY_SCALE)
            scaled[here] = ic2
            scaled_e[here] = ic2 * e
            twice[here] = e * (1.0 / CAUCHY_SCALE)

        loop(height, BLOCK, prepare)

    def product(i0):
        here = pl.ds(i0, BLOCK)
        t1[pl.ds(i0 + RADIUS, BLOCK)] = col_box(est[here] * s_ref[here])

    loop(height, BLOCK, product)

    def fit(i0):
        here = pl.ds(i0, BLOCK)
        cross = row_box(t1[pl.ds(i0, BLOCK + 8)])
        mean = mean_ref[here]
        slope = cross * gain[here] - mean * mgain[here]
        offset = mean - slope * guide[here]
        t2[pl.ds(i0 + RADIUS, BLOCK)] = col_box(slope)
        t3[pl.ds(i0 + RADIUS, BLOCK)] = col_box(offset)

    loop(height, BLOCK, fit)

    def weigh(i0):
        here = pl.ds(i0, BLOCK)
        a = row_box(t2[pl.ds(i0, BLOCK + 8)])
        b = row_box(t3[pl.ds(i0, BLOCK + 8)])
        gap = (a * scaled_e[here] + b * scaled[here]) - twice[here]
        weight = 1.0 / (1.0 + gap * gap)
        acc_w[here] += weight * s_ref[here]
        acc_t[here] += weight

    loop(height, BLOCK, weigh)

    @pl.when(g == pl.num_programs(0) - 1)
    def _():
        dest = flat if last else out_ref

        def finish(i0):
            here = pl.ds(i0, BLOCK)
            w = jnp.sum(acc_w[here], axis=1)
            t = jnp.sum(acc_t[here], axis=1)
            dest[here, :] = w / t

        loop(height, BLOCK, finish)
        if last:
            rows = height // n_row
            half = rows // 2
            low = lane_ids((half, LANES)) < 64
            for r in range(n_row):
                a = flat[rows * r : rows * r + half, :]
                b = flat[rows * r + half : rows * (r + 1), :]
                v = jnp.where(low, roll(a, -32), roll(b, 32))
                for f in range(n_frame):
                    out_ref[f, r] = v


def rows_kernel(r_ref, out_ref):
    half = r_ref.shape[1]
    low = lane_ids((half, LANES)) < 64
    for k in range(r_ref.shape[0] // 2):
        a, b = r_ref[2 * k], r_ref[2 * k + 1]
        here = slice(k * LANES, (k + 1) * LANES)
        out_ref[0:half, here] = jnp.where(low, a, roll(b, 64))
        out_ref[half : 2 * half, here] = jnp.where(low, roll(a, 64), b)


def strip_program(frames):
    n_frame, n_row = lax.axis_size("frame"), lax.axis_size("row")
    n_dev = n_frame * n_row
    local, rows, width = frames.shape
    height = rows * n_row
    half = rows // 2
    f32 = jnp.float32

    def strip():
        return lax.axis_index("frame") * n_row + lax.axis_index("row")

    packed = pl.pallas_call(
        functools.partial(pack_kernel, rows),
        grid=(width // LANES,),
        in_specs=[pl.BlockSpec((local * rows, LANES), lambda k: (0, k))],
        out_specs=pl.BlockSpec((2, half, GROUP, LANES), lambda k: (k, 0, 0, 0)),
        out_shape=jax.ShapeDtypeStruct((n_dev, half, GROUP, LANES), f32),
        name="pack",
    )(frames.reshape(local * rows, width))

    got = lax.all_to_all(packed, BOTH, 0, 0, tiled=True)

    tile = jax.ShapeDtypeStruct((height, n_frame * GROUP, LANES), f32)
    edge = jax.ShapeDtypeStruct((height // 16, n_frame * GROUP, LANES), f32)
    tile_spec = pl.BlockSpec((height, GROUP, LANES), lambda g: (0, g, 0))
    edge_spec = pl.BlockSpec((height // 16, GROUP, LANES), lambda g: (0, g, 0))
    field = pltpu.VMEM((height, GROUP, LANES), f32)
    padded = pltpu.VMEM((height + 2 * RADIUS, GROUP, LANES), f32)
    flat_spec = pl.BlockSpec((height, LANES), lambda g: (0, 0))
    flat = jax.ShapeDtypeStruct((height, LANES), f32)

    centre, left_edge, right_edge = pl.pallas_call(
        functools.partial(unpack_kernel, rows),
        grid=(n_frame,),
        in_specs=[pl.BlockSpec((n_row, half, GROUP, LANES), lambda g: (g, 0, 0, 0))],
        out_specs=(tile_spec, edge_spec, edge_spec),
        out_shape=(tile, edge, edge),
        name="unpack",
    )(got)

    up = [(i, i + 1) for i in range(n_dev - 1)]
    down = [(j, i) for i, j in up]

    def swap(to_left, to_right):
        return lax.ppermute(to_right, BOTH, up), lax.ppermute(to_left, BOTH, down)

    before, after = swap(left_edge, right_edge)
    full, mean, est = pl.pallas_call(
        functools.partial(stats_kernel, width, strip),
        grid=(n_frame,),
        in_specs=[tile_spec, edge_spec, edge_spec],
        out_specs=(tile_spec, tile_spec, flat_spec),
        out_shape=(tile, tile, flat),
        scratch_shapes=[padded, field],
        name="stats",
    )(centre, before, after)

    for k in range(ROUNDS):
        last = k == ROUNDS - 1
        before, after = swap(est, est) if k else (est, est)
        if last:
            out_shape = jax.ShapeDtypeStruct((n_frame, n_row, half, LANES), f32)
            out_spec = pl.BlockSpec(out_shape.shape, lambda g: (0, 0, 0, 0))
        else:
            out_shape, out_spec = flat, flat_spec
        est = pl.pallas_call(
            functools.partial(round_kernel, width, strip, k > 0, last, n_frame, n_row),
            grid=(n_frame,),
            in_specs=[flat_spec, flat_spec, flat_spec, tile_spec, tile_spec],
            out_specs=out_spec,
            out_shape=out_shape,
            scratch_shapes=[field] * 7 + [padded] * 3 + [field] * 2
            + [pltpu.VMEM((height, LANES), f32)],
            name="round",
        )(est, before, after, full, mean)

    got = lax.all_to_all(est.reshape(n_dev, half, LANES), BOTH, 0, 0, tiled=True)
    return pl.pallas_call(
        rows_kernel,
        out_shape=jax.ShapeDtypeStruct((rows, width), f32),
        name="rows",
    )(got)


def with_halo(x, dim, width):
    n, length = lax.axis_size("row"), x.shape[dim]
    up = [(i, i + 1) for i in range(n - 1)]
    down = [(j, i) for i, j in up]
    before = lax.ppermute(lax.slice_in_dim(x, length - width, length, axis=dim), "row", up)
    after = lax.ppermute(lax.slice_in_dim(x, 0, width, axis=dim), "row", down)
    return jnp.concatenate([before, x, after], axis=dim)


def smooth(padded_rows, area):
    length, width = padded_rows.shape[-2] - 8, padded_rows.shape[-1]
    total = sum(padded_rows[..., k : k + length, :] for k in range(9))
    padded = jnp.pad(total, [(0, 0)] * (total.ndim - 1) + [(4, 4)])
    return sum(padded[..., k : k + width] for k in range(9)) / area


def row_program(frames):
    rows, width = frames.shape[1:]
    height = rows * lax.axis_size("row")
    start = lax.axis_index("row") * rows
    total_frames = frames.shape[0] * lax.axis_size("frame")
    area = (
        count(start + jnp.arange(rows, dtype=jnp.int32), height)[:, None]
        * count(jnp.arange(width, dtype=jnp.int32), width)[None, :]
    )
    estimate = lax.psum(jnp.sum(frames, axis=0), "frame") / total_frames
    padded_frames = with_halo(frames, 1, 4)
    mean_frame = smooth(padded_frames, area)
    for _ in range(ROUNDS):
        padded = with_halo(estimate, 0, 4)
        guide = smooth(padded, area)
        variance = smooth(padded * padded, area) - guide * guide
        cross = smooth(padded[None] * padded_frames, area)
        slope = (cross - guide * mean_frame) / (variance + GUIDE_EPS)
        offset = mean_frame - slope * guide
        stacked = with_halo(jnp.stack((slope, offset)), 2, 4)
        filtered = smooth(stacked[0], area) * estimate[None] + smooth(stacked[1], area)
        gap = (filtered - estimate[None]) / CAUCHY_SCALE
        weight = 1.0 / (1.0 + gap * gap)
        sums = lax.psum((jnp.sum(weight * frames, axis=0), jnp.sum(weight, axis=0)), "frame")
        estimate = sums[0] / sums[1]
    return estimate


def shards(frames):
    local, rows, width = frames.shape
    n_dev = lax.axis_size("frame") * lax.axis_size("row")
    if local == GROUP and width == 64 * n_dev and rows % 16 == 0:
        return strip_program(frames)
    return row_program(frames)


def solution(mesh):
    return jax.shard_map(
        shards,
        mesh=mesh,
        in_specs=(P("frame", "row", None),),
        out_specs=P("row", None),
        check_vma=False,
    )
```

time: 472 us -> 322 us (0.68); the launches traced: 465 us -> 321 us
  waiting for transfers between devices: 328 us -> 6.19 us
  Pallas kernels: 0 us -> 217 us
  other arithmetic: 87.1 us -> 0 us
  blocking collectives: 0 us -> 78.7 us
  between operations: 14.2 us -> 0.09 us
  starting transfers between devices: 30.6 us -> 17.7 us
    psum x4 -> x0, waiting for transfers between devices: 309 us -> none  [the longest x3 233 us: shards(): sums = lax.psum((weighted, total), 'frame')]
    pallas_call x0 -> x7, Pallas kernels: none -> 217 us  [the longest x3 172 us: strip_program(): pl.pallas_call(functools.partial(round_kernel, width, strip, k > 0, last,...]
    all_to_all x0 -> x2, blocking collectives: none -> 78.7 us  [the longest x1 56.1 us: strip_program(): got = lax.all_to_all(packed, BOTH, 0, 0, tiled=True)]
    reduce_sum x3 -> x0, other arithmetic: 29.1 us -> none  [shards(): total = jnp.sum(weight, axis=0)]
    add x18 -> x0, other arithmetic: 23.9 us -> none  [the longest x15 19.8 us: row_sum(): total = total + field[..., offset:offset + length, :]]
    another operation x3 -> x0, other arithmetic: 23.9 us -> none  [shards(): stacked = with_halo(jnp.stack((slope, offset_term)), (('row', 2),), 4)]
    ppermute x14 -> x6, waiting for transfers between devices: 19.1 us -> 6.19 us  [swap(): return (lax.ppermute(to_right, BOTH, up), lax.ppermute(to_left, BOTH, down))]
    ppermute x14 -> x6, starting transfers between devices: 30.4 us -> 17.7 us  [swap(): return (lax.ppermute(to_right, BOTH, up), lax.ppermute(to_left, BOTH, down))]
  transfers between devices with their start and end apart: 18 -> 6, of which waited for: 11 -> 3; matrix products, arithmetic and copies ran while one was open for 0% -> 0% of each run, Pallas kernels for 0% -> 0%
where the time goes in v1:
time: 322 us; the launch traced here: 321 us
  Pallas kernels  217 us (67%)
  blocking collectives  78.7 us (24%)
  starting transfers between devices  17.7 us (5%)
  waiting for transfers between devices  6.19 us (2%)
    pallas_call x3, Pallas kernels, strip_program(): pl.pallas_call(functools.partial(round_kernel, width, strip, k > 0, last,...  172 us
    all_to_all x1, blocking collectives, strip_program(): got = lax.all_to_all(packed, BOTH, 0, 0, tiled=True)  56.1 us
    pallas_call x1, Pallas kernels, strip_program(): pl.pallas_call(functools.partial(stats_kernel, width, strip), grid=(n_fra...  24.4 us
    all_to_all x1, blocking collectives, strip_program(): lax.all_to_all(est.reshape(n_dev, half, LANES), BOTH, 0, 0, tiled=True)  22.6 us
    ppermute x6, starting transfers between devices, swap(): return (lax.ppermute(to_right, BOTH, up), lax.ppermute(to_left, BOTH, down))  17.7 us
    pallas_call x1, Pallas kernels, strip_program(): pl.pallas_call(functools.partial(pack_kernel, rows), grid=(width // LANES...  10.2 us
    pallas_call x1, Pallas kernels, strip_program(): pl.pallas_call(functools.partial(unpack_kernel, rows), grid=(n_frame,), i...  7.71 us
  transfers between devices with their start and end apart: 6, of which 3 were waited for; matrix products, arithmetic and copies ran while one was open for 0% of the time, Pallas kernels for 0%

profile of v1, /device:TPU:0, one launch (start us, length us, event | category | flops | bytes accessed | tf_op | source)
XLA Modules:
  0.0 321.2 jit_solution(17007318473418006343)
XLA Ops:
  0.0 10.2 %pack.1 = f32[32,16,8,128]{3,2,1,0:T(8,128)} custom-call(f32[256,2048]{1,0:T(8,128)} %bitcast.2), custom_call_target="tpu_custom_call" | custom-call | tf_op jit(solution)/shard_map/pack/pallas_call | solution.py:267
  10.2 56.1 %all_to_all.10.r_ref = f32[32,16,8,128]{3,2,1,0:T(8,128)} all-to-all(f32[32,16,8,128]{3,2,1,0:T(8,128)} %pack.1), channel_id=1, replica_groups=mesh['frame'=8,'row'=4] {'frame','row'}, dimensions={0} | all-to-all | bytes 4194304 | tf_op jit(solution)/shard_map/all_to_all | solution.py:276
  66.3 7.7 %unpack.1 = (f32[128,64,128]{2,1,0:T(8,128)}, f32[8,64,128]{2,1,0:T(8,128)}, f32[8,64,128]{2,1,0:T(8,128)}) custom-call(f32[32,16,8,128]{3,2,1,0:T(8,128)} %all_to_all.10.r_ref), custom_call_target="tpu_custom_call" | custom-call | tf_op jit(solution)/shard_map/unpack/pallas_call | solution.py:287
  74.0 1.3 collective-permute-start
  75.3 1.3 collective-permute-start.1
  76.6 0.0 collective-permute-done.before_ref
  76.7 0.0 copy-start
  76.7 4.0 %collective-permute-done.1.after_ref = f32[8,64,128]{2,1,0:T(8,128)S(1)} collective-permute-done((f32[8,64,128]{2,1,0:T(8,128)}, f32[8,64,128]{2,1,0:T(8,128)S(1)}, u32[]{:S(2)}, u32[]{:S(2)}) %collective-permute-start.1) | collective-permute-done | bytes 262176 | tf_op jit(solution)/shard_map/ppermute | solution.py:300
  80.7 0.0 copy-start.1
  80.7 0.0 copy-done
  80.7 0.7 copy-done.1
  81.4 24.4 %stats.1 = (f32[128,64,128]{2,1,0:T(8,128)}, f32[128,64,128]{2,1,0:T(8,128)}, f32[128,128]{1,0:T(8,128)}) custom-call(f32[128,64,128]{2,1,0:T(8,128)} %get-tuple-element.11.s_ref, f32[8,64,128]{2,1,0:T(8,128)} %copy-done, f32[8,64,128]{2,1,0:T(8,128)} %copy-done.1), custom_call_target="tpu_custom_call" | custom-call | tf_op jit(solution)/shard_map/stats/pallas_call | solution.py:303
  105.8 57.1 %round.3.e_ref = f32[128,128]{1,0:T(8,128)} custom-call(f32[128,128]{1,0:T(8,128)} %get-tuple-element.14.e_ref.before_ref.after_ref, f32[128,128]{1,0:T(8,128)} %get-tuple-element.14.e_ref.before_ref.after_ref, f32[128,128]{1,0:T(8,128)} %get-tuple-element.14.e_ref.before_ref.after_ref, f32[128,64,128]{2,1,0:T(8,128)} %get-tuple-element.15.s_ref, ...), custom_call_target="tpu_custom_call" | custom-call | tf_op jit(solution)/shard_map/round/pallas_call | solution.py:321
  162.9 1.3 collective-permute-start.3
  164.1 7.3 %collective-permute-start.2 = (f32[128,128]{1,0:T(8,128)}, f32[128,128]{1,0:T(8,128)S(1)}, u32[]{:S(2)}, u32[]{:S(2)}) collective-permute-start(f32[128,128]{1,0:T(8,128)} %round.3.e_ref), channel_id=1, source_target_pairs={{0,1},{1,2},{2,3},{3,4},{4,5},{5,6},{6,7},{7,8},{8,9},{9,10},{10,1... | collective-permute-start | bytes 196616 | tf_op jit(solution)/shard_map/ppermute | solution.py:300
  171.4 0.0 collective-permute-done.3.after_ref
  171.5 0.0 copy-start.3
  171.5 1.1 collective-permute-done.2.before_ref
  172.5 0.0 copy-done.3
  172.5 0.6 copy-done.5
  173.2 57.6 %round.4.e_ref = f32[128,128]{1,0:T(8,128)} custom-call(f32[128,128]{1,0:T(8,128)} %round.3.e_ref, f32[128,128]{1,0:T(8,128)} %copy-done.5, f32[128,128]{1,0:T(8,128)} %copy-done.3, f32[128,64,128]{2,1,0:T(8,128)} %get-tuple-element.15.s_ref, f32[128,64,128]{2,1,0:T(8,128)} %get-tuple-element.16.mean_ref), custom_call_target="tpu_custom_call" | custom-call | tf_op jit(solution)/shard_map/round/pallas_call | solution.py:321
  230.8 1.3 collective-permute-start.5
  232.1 5.3 %collective-permute-start.4 = (f32[128,128]{1,0:T(8,128)}, f32[128,128]{1,0:T(8,128)S(1)}, u32[]{:S(2)}, u32[]{:S(2)}) collective-permute-start(f32[128,128]{1,0:T(8,128)} %round.4.e_ref), channel_id=1, source_target_pairs={{0,1},{1,2},{2,3},{3,4},{4,5},{5,6},{6,7},{7,8},{8,9},{9,10},{10,1... | collective-permute-start | bytes 196616 | tf_op jit(solution)/shard_map/ppermute | solution.py:300
  237.4 0.0 collective-permute-done.5.after_ref
  237.4 0.0 copy-start.2
  237.4 1.1 collective-permute-done.4.before_ref
  238.4 0.0 copy-done.2
  238.4 0.0 copy-start.4
  238.4 0.6 copy-done.4
  239.1 57.8 %round.5 = f32[8,4,16,128]{3,2,1,0:T(8,128)} custom-call(f32[128,128]{1,0:T(8,128)} %round.4.e_ref, f32[128,128]{1,0:T(8,128)} %copy-done.4, f32[128,128]{1,0:T(8,128)} %copy-done.2, f32[128,64,128]{2,1,0:T(8,128)} %get-tuple-element.15.s_ref, f32[128,64,128]{2,1,0:T(8,128)} %get-tuple-element.16.mean_ref), custom_call_target="tpu_custom_call" | custom-call | tf_op jit(solution)/shard_map/round/pallas_call | solution.py:321
  296.9 22.6 %all_to_all.11.r_ref = f32[32,16,128]{2,1,0:T(8,128)} all-to-all(f32[32,16,128]{2,1,0:T(8,128)} %bitcast.3), channel_id=1, replica_groups=mesh['frame'=8,'row'=4] {'frame','row'}, dimensions={0} | all-to-all | bytes 524288 | tf_op jit(solution)/shard_map/all_to_all | solution.py:332
  319.4 1.8 rows.1
  (1 shorter events, 0.0 us)
Async XLA Ops:
  74.0 2.6 collective-permute-start
  75.3 5.3 %collective-permute-start.1 = (f32[8,64,128]{2,1,0:T(8,128)}, f32[8,64,128]{2,1,0:T(8,128)S(1)}, u32[]{:S(2)}, u32[]{:S(2)}) collective-permute-start(f32[8,64,128]{2,1,0:T(8,128)} %get-tuple-element.13), channel_id=1, source_target_pairs={{1,0},{2,1},{3,2},{4,3},{5,4},{6,5},{7,6},{8,7},{9,8},{10,9},{11,1... | collective-permute-start | bytes 786440 | tf_op jit(solution)/shard_map/ppermute | solution.py:300
  76.7 4.0 %copy-start = (f32[8,64,128]{2,1,0:T(8,128)}, f32[8,64,128]{2,1,0:T(8,128)S(1)}, u32[]{:S(2)}) copy-start(f32[8,64,128]{2,1,0:T(8,128)S(1)} %collective-permute-done.before_ref) | copy-start | bytes 786436
  80.7 0.7 copy-start.1
  162.9 8.6 %collective-permute-start.3 = (f32[128,128]{1,0:T(8,128)}, f32[128,128]{1,0:T(8,128)S(1)}, u32[]{:S(2)}, u32[]{:S(2)}) collective-permute-start(f32[128,128]{1,0:T(8,128)} %round.3.e_ref), channel_id=1, source_target_pairs={{1,0},{2,1},{3,2},{4,3},{5,4},{6,5},{7,6},{8,7},{9,8},{10,9},{11,1... | collective-permute-start | bytes 196616 | tf_op jit(solution)/shard_map/ppermute | solution.py:300
  164.1 8.4 %collective-permute-start.2 = (f32[128,128]{1,0:T(8,128)}, f32[128,128]{1,0:T(8,128)S(1)}, u32[]{:S(2)}, u32[]{:S(2)}) collective-permute-start(f32[128,128]{1,0:T(8,128)} %round.3.e_ref), channel_id=1, source_target_pairs={{0,1},{1,2},{2,3},{3,4},{4,5},{5,6},{6,7},{7,8},{8,9},{9,10},{10,1... | collective-permute-start | bytes 196616 | tf_op jit(solution)/shard_map/ppermute | solution.py:300
  171.5 1.1 copy-start.3
  172.5 0.6 copy-start.5
  230.8 6.6 %collective-permute-start.5 = (f32[128,128]{1,0:T(8,128)}, f32[128,128]{1,0:T(8,128)S(1)}, u32[]{:S(2)}, u32[]{:S(2)}) collective-permute-start(f32[128,128]{1,0:T(8,128)} %round.4.e_ref), channel_id=1, source_target_pairs={{1,0},{2,1},{3,2},{4,3},{5,4},{6,5},{7,6},{8,7},{9,8},{10,9},{11,1... | collective-permute-start | bytes 196616 | tf_op jit(solution)/shard_map/ppermute | solution.py:300
  232.1 6.4 %collective-permute-start.4 = (f32[128,128]{1,0:T(8,128)}, f32[128,128]{1,0:T(8,128)S(1)}, u32[]{:S(2)}, u32[]{:S(2)}) collective-permute-start(f32[128,128]{1,0:T(8,128)} %round.4.e_ref), channel_id=1, source_target_pairs={{0,1},{1,2},{2,3},{3,4},{4,5},{5,6},{6,7},{7,8},{8,9},{9,10},{10,1... | collective-permute-start | bytes 196616 | tf_op jit(solution)/shard_map/ppermute | solution.py:300
  237.4 1.1 copy-start.2
  238.4 0.6 copy-start.4

commit v2 on v0

v2 whole, which is shorter than its diff:
```python
import functools

import jax
import jax.numpy as jnp
from jax import lax
from jax.experimental import pallas as pl
from jax.experimental.pallas import tpu as pltpu
from jax.sharding import PartitionSpec as P

ROUNDS = 3
RADIUS = 4
GUIDE_EPS = 0.05
CAUCHY_SCALE = 0.5

LANES = 128
GROUP = 8
BOTH = ("frame", "row")


HALO = 2 * RADIUS
HALF = LANES // 2


def lane_ids(shape):
    return lax.broadcasted_iota(jnp.int32, shape, len(shape) - 1)


def roll(x, shift):
    return pltpu.roll(x, shift % LANES, x.ndim - 1)


def row_box(v):
    n = v.shape[0]
    s3 = v[0 : n - 2] + v[1 : n - 1] + v[2:n]
    return s3[0 : n - 8] + s3[3 : n - 5] + s3[6 : n - 2]


def col_box(ref, at, tmp):
    n = ref.shape[1] - HALO
    tmp[0 : n + 6] = ref[at, 0 : n + 6] + ref[at, 1 : n + 7] + ref[at, 2 : n + 8]
    return tmp[0:n] + tmp[3 : n + 3] + tmp[6 : n + 6]


def count(place, limit):
    lower = jnp.maximum(place - RADIUS, 0)
    upper = jnp.minimum(place + RADIUS, limit - 1)
    return jnp.maximum(upper - lower + 1, 1).astype(jnp.float32)


def loop(total, step, body):
    def go(i, carry):
        body(i * step)
        return carry

    lax.fori_loop(0, total // step, go, 0)


def halves_matrix():
    shape = (LANES, LANES)
    row = lax.broadcasted_iota(jnp.int32, shape, 0)
    return jnp.where((row < HALF) == (lane_ids(shape) < HALF), 1.0, 0.0).astype(jnp.bfloat16)


def frame_sum(x, ones):
    total = None
    for _ in range(3):
        part = x.astype(jnp.bfloat16)
        x = x - part.astype(jnp.float32)
        term = jnp.dot(part, ones, preferred_element_type=jnp.float32)
        total = term if total is None else total + term
    return total


def row_halo(ref, rows):
    width = ref.shape[1]
    lane = lane_ids((width, LANES))
    for k in range(HALO):
        ref[k] = jnp.where(lane >= HALF, roll(ref[rows + k], HALF), 0.0)
        ref[HALO + rows + k] = jnp.where(lane < HALF, roll(ref[HALO + k], HALF), 0.0)


def pack_kernel(rows, x_ref, out_ref, tmp):
    half = rows // 2
    low = lane_ids((GROUP, LANES)) < HALF
    for f in range(GROUP):
        tmp[f * (rows + 1) : f * (rows + 1) + rows] = x_ref[f * rows : (f + 1) * rows, :]
    for i in range(half):
        a = tmp[pl.ds(i, GROUP, stride=rows + 1), :]
        b = tmp[pl.ds(i + half, GROUP, stride=rows + 1), :]
        out_ref[0, i] = jnp.where(low, a, roll(b, HALF))
        out_ref[1, i] = jnp.where(low, roll(a, HALF), b)


def unpack_kernel(rows, r_ref, s_ref, left_ref, right_ref):
    groups, n_row, half = r_ref.shape[0:3]
    for r in range(n_row // 2):

        def go(i):
            parts = [r_ref[g, r + h * (n_row // 2), i] for h in range(2) for g in range(groups)]
            v = jnp.transpose(jnp.concatenate(parts, axis=0))
            for k in range(2):
                at = r * rows + k * half + i
                s_ref[at] = v[k * HALF : (k + 1) * HALF]
                left_ref[at] = v[k * HALF : k * HALF + HALO]
                right_ref[at] = v[(k + 1) * HALF - HALO : (k + 1) * HALF]

        loop(half, 1, go)


def stats_kernel(
    width, strip, s_ref, before_ref, after_ref, full_ref, mean_ref, area_ref, est_ref, boxed, tmp
):
    rows, cols = s_ref.shape[0:2]
    wide = cols + HALO
    height = 2 * rows
    first_col = strip() * cols - RADIUS
    ones = halves_matrix()

    def place(q):
        full_ref[q + HALO, 0:HALO] = before_ref[q]
        full_ref[q + HALO, HALO : HALO + cols] = s_ref[q]
        full_ref[q + HALO, HALO + cols :] = after_ref[q]

    loop(rows, 1, place)
    row_halo(full_ref, rows)

    def first(q):
        est_ref[q] = frame_sum(full_ref[q], ones) / HALF

    loop(rows + 2 * HALO, 1, first)

    step = rows // 8 * 3

    def down(q):
        for j in range(0, cols + 2 * HALO, 8):
            boxed[pl.ds(q, step), j : j + 8] = row_box(full_ref[pl.ds(q, step + HALO), j : j + 8])

    loop(rows + HALO, step, down)

    col = first_col + lax.broadcasted_iota(jnp.int32, (wide, LANES), 0)
    upper = jnp.where(lane_ids((wide, LANES)) < HALF, 0, rows)
    col_inverse = jnp.where(
        jnp.logical_and(col >= 0, col < width), 1.0 / count(col, width), 0.0
    )

    def means(q):
        row = q - RADIUS + upper
        inside = jnp.logical_and(row >= 0, row < height)
        area = jnp.where(inside, col_inverse / count(row, height), 0.0)
        area_ref[q] = area
        mean_ref[q] = col_box(boxed, q, tmp) * area

    loop(rows + HALO, 1, means)


def round_kernel(first, last, n_frame, n_row, *refs):
    e_ref, before_ref, after_ref, s_ref, mean_ref, area_ref = refs[0:6]
    outs, scratch = (refs[6:7], refs[7:]) if last else (refs[6:9], refs[9:])
    ext, b1, b2, b3, slope, offset, tmp, flat = scratch
    rows = mean_ref.shape[0] - HALO
    cols = mean_ref.shape[1] - HALO
    ones = halves_matrix()
    est = e_ref if first else ext
    edge_row = lane_ids((HALO, LANES)) % HALF

    if not first:
        def place(q):
            here = edge_row == q
            ext[q + HALO, 0:HALO] = frame_sum(jnp.where(here, before_ref[...], 0.0), ones)
            ext[q + HALO, HALO : HALO + cols] = e_ref[q]
            ext[q + HALO, HALO + cols :] = frame_sum(jnp.where(here, after_ref[...], 0.0), ones)

        loop(rows, 1, place)
        row_halo(ext, rows)

    step = rows // 8 * 3

    def down(q):
        for j in range(0, cols + 2 * HALO, 8):
            e = est[pl.ds(q, step + HALO), j : j + 8]
            b1[pl.ds(q, step), j : j + 8] = row_box(e * s_ref[pl.ds(q, step + HALO), j : j + 8])
            b2[pl.ds(q, step), j : j + 8] = row_box(e)
            b3[pl.ds(q, step), j : j + 8] = row_box(e * e)

    loop(rows + HALO, step, down)

    def fit(q0):
        for k in range(2):
            q = q0 + k
            area, mean = area_ref[q], mean_ref[q]
            guide = col_box(b2, q, tmp.at[3 * k]) * area
            variance = col_box(b3, q, tmp.at[3 * k + 1]) * area - guide * guide
            cross = col_box(b1, q, tmp.at[3 * k + 2]) * area
            a = (cross - guide * mean) / (variance + GUIDE_EPS)
            slope[q] = a
            offset[q] = mean - a * guide

    loop(rows + HALO, 2, fit)

    block = rows // 4

    def down_again(q):
        for j in range(0, cols + HALO, 8):
            b1[pl.ds(q, block), j : j + 8] = row_box(slope[pl.ds(q, block + HALO), j : j + 8])
            b2[pl.ds(q, block), j : j + 8] = row_box(offset[pl.ds(q, block + HALO), j : j + 8])

    loop(rows, block, down_again)

    lane = edge_row[0:1]

    def weigh(q0):
        for k in range(2):
            q = q0 + k
            area = area_ref[q + RADIUS, RADIUS : RADIUS + cols]
            e = est[q + HALO, HALO : HALO + cols]
            p = s_ref[q + HALO, HALO : HALO + cols]
            a = col_box(b1.at[:, 0 : cols + HALO], q, tmp.at[2 * k])
            b = col_box(b2.at[:, 0 : cols + HALO], q, tmp.at[2 * k + 1])
            gap = ((a * e + b) * area - e) * (1.0 / CAUCHY_SCALE)
            weight = 1.0 / (1.0 + gap * gap)
            new = frame_sum(weight * p, ones) / frame_sum(weight, ones)
            if last:
                flat[...] = jnp.where(lane == q, new, flat[...])
            else:
                outs[0][q] = new
                here = edge_row == q
                outs[1][...] = jnp.where(here, new[0:HALO], outs[1][...])
                outs[2][...] = jnp.where(here, new[cols - HALO :], outs[2][...])

    if last:
        flat[...] = jnp.zeros_like(flat)
    else:
        outs[1][...] = jnp.zeros_like(outs[1])
        outs[2][...] = jnp.zeros_like(outs[2])
    loop(rows, 2, weigh)

    if last:
        shard = 2 * rows // n_row
        half = shard // 2
        turned = jnp.transpose(jnp.concatenate([flat[...], roll(flat[...], -half)], axis=0))
        for r in range(n_row):
            for f in range(n_frame):
                outs[0][f, r] = turned[r * shard : r * shard + half]


def rows_kernel(r_ref, out_ref):
    half = r_ref.shape[1]
    low = lane_ids((half, LANES)) < HALF
    for k in range(r_ref.shape[0] // 2):
        a, b = r_ref[2 * k], r_ref[2 * k + 1]
        here = slice(k * LANES, (k + 1) * LANES)
        out_ref[0:half, here] = jnp.where(low, a, roll(b, HALF))
        out_ref[half : 2 * half, here] = jnp.where(low, roll(a, HALF), b)


def strip_program(frames):
    n_frame, n_row = lax.axis_size("frame"), lax.axis_size("row")
    n_dev = n_frame * n_row
    local, rows, width = frames.shape
    half = rows // 2
    deep = rows * n_row // 2
    cols = width // n_dev
    f32 = jnp.float32

    def array(*shape):
        return jax.ShapeDtypeStruct(shape + (LANES,), f32)

    def scratch(*shape):
        return pltpu.VMEM(shape + (LANES,), f32)

    def strip():
        return lax.axis_index("frame") * n_row + lax.axis_index("row")

    packed = pl.pallas_call(
        functools.partial(pack_kernel, rows),
        grid=(width // LANES,),
        in_specs=[pl.BlockSpec((local * rows, LANES), lambda k: (0, k))],
        out_specs=pl.BlockSpec((2, half, GROUP, LANES), lambda k: (k, 0, 0, 0)),
        out_shape=array(n_dev, half, GROUP),
        scratch_shapes=[scratch(GROUP * (rows + 1))],
        name="pack",
    )(frames.reshape(local * rows, width))

    got = lax.all_to_all(packed, BOTH, 0, 0, tiled=True)

    edge = array(deep, HALO)
    centre, left_edge, right_edge = pl.pallas_call(
        functools.partial(unpack_kernel, rows),
        out_shape=(array(deep, cols), edge, edge),
        name="unpack",
    )(got.reshape(n_frame, n_row, half, GROUP, LANES))

    up = [(i, i + 1) for i in range(n_dev - 1)]
    down = [(j, i) for i, j in up]

    def swap(to_left, to_right):
        return lax.ppermute(to_right, BOTH, up), lax.ppermute(to_left, BOTH, down)

    before, after = swap(left_edge, right_edge)
    whole = (deep + 2 * HALO, cols + 2 * HALO)
    fitted = (deep + HALO, cols + HALO)
    full, mean, area, est = pl.pallas_call(
        functools.partial(stats_kernel, width, strip),
        out_shape=(array(*whole), array(*fitted), array(*fitted), array(*whole)),
        scratch_shapes=[scratch(fitted[0], whole[1]), scratch(whole[1])],
        name="stats",
    )(centre, before, after)

    before = after = jnp.zeros((HALO, LANES), f32)
    for k in range(ROUNDS):
        first, last = k == 0, k == ROUNDS - 1
        if not first:
            before, after = swap(left_edge, right_edge)
        if last:
            out_shape = array(n_frame, n_row, half)
        else:
            out_shape = (array(deep, cols), array(HALO), array(HALO))
        result = pl.pallas_call(
            functools.partial(round_kernel, first, last, n_frame, n_row),
            out_shape=out_shape,
            scratch_shapes=[scratch(*whole)]
            + [scratch(fitted[0], whole[1])] * 3
            + [scratch(*fitted)] * 2
            + [scratch(6, whole[1]), scratch(cols)],
            name="round",
        )(est, before, after, full, mean, area)
        if not last:
            est, left_edge, right_edge = result

    got = lax.all_to_all(result.reshape(n_dev, half, LANES), BOTH, 0, 0, tiled=True)
    return pl.pallas_call(
        rows_kernel,
        out_shape=jax.ShapeDtypeStruct((rows, width), f32),
        name="rows",
    )(got)


def with_halo(x, dim, width):
    n, length = lax.axis_size("row"), x.shape[dim]
    up = [(i, i + 1) for i in range(n - 1)]
    down = [(j, i) for i, j in up]
    before = lax.ppermute(lax.slice_in_dim(x, length - width, length, axis=dim), "row", up)
    after = lax.ppermute(lax.slice_in_dim(x, 0, width, axis=dim), "row", down)
    return jnp.concatenate([before, x, after], axis=dim)


def smooth(padded_rows, area):
    length, width = padded_rows.shape[-2] - 8, padded_rows.shape[-1]
    total = sum(padded_rows[..., k : k + length, :] for k in range(9))
    padded = jnp.pad(total, [(0, 0)] * (total.ndim - 1) + [(4, 4)])
    return sum(padded[..., k : k + width] for k in range(9)) / area


def row_program(frames):
    rows, width = frames.shape[1:]
    height = rows * lax.axis_size("row")
    start = lax.axis_index("row") * rows
    total_frames = frames.shape[0] * lax.axis_size("frame")
    area = (
        count(start + jnp.arange(rows, dtype=jnp.int32), height)[:, None]
        * count(jnp.arange(width, dtype=jnp.int32), width)[None, :]
    )
    estimate = lax.psum(jnp.sum(frames, axis=0), "frame") / total_frames
    padded_frames = with_halo(frames, 1, 4)
    mean_frame = smooth(padded_frames, area)
    for _ in range(ROUNDS):
        padded = with_halo(estimate, 0, 4)
        guide = smooth(padded, area)
        variance = smooth(padded * padded, area) - guide * guide
        cross = smooth(padded[None] * padded_frames, area)
        slope = (cross - guide * mean_frame) / (variance + GUIDE_EPS)
        offset = mean_frame - slope * guide
        stacked = with_halo(jnp.stack((slope, offset)), 2, 4)
        filtered = smooth(stacked[0], area) * estimate[None] + smooth(stacked[1], area)
        gap = (filtered - estimate[None]) / CAUCHY_SCALE
        weight = 1.0 / (1.0 + gap * gap)
        sums = lax.psum((jnp.sum(weight * frames, axis=0), jnp.sum(weight, axis=0)), "frame")
        estimate = sums[0] / sums[1]
    return estimate


def shards(frames):
    local, rows, width = frames.shape
    n_dev = lax.axis_size("frame") * lax.axis_size("row")
    strips = local == GROUP and local * lax.axis_size("frame") == LANES // 2
    strips = strips and 2 * width == LANES * n_dev and rows % 16 == 0
    strips = strips and rows * lax.axis_size("row") % LANES == 0 and lax.axis_size("row") % 2 == 0
    if strips and rows * lax.axis_size("row") == LANES:
        return strip_program(frames)
    return row_program(frames)


def solution(mesh):
    return jax.shard_map(
        shards,
        mesh=mesh,
        in_specs=(P("frame", "row", None),),
        out_specs=P("row", None),
        check_vma=False,
    )
```

time: 472 us -> 225 us (0.48); the launches traced: 465 us -> 225 us
  waiting for transfers between devices: 328 us -> 7.94 us
  Pallas kernels: 0 us -> 122 us
  other arithmetic: 87.1 us -> 0 us
  blocking collectives: 0 us -> 75.6 us
  starting transfers between devices: 30.6 us -> 16.3 us
  between operations: 14.2 us -> 0.09 us
    psum x4 -> x0, waiting for transfers between devices: 309 us -> none  [the longest x3 233 us: shards(): sums = lax.psum((weighted, total), 'frame')]
    pallas_call x0 -> x7, Pallas kernels: none -> 122 us  [the longest x3 81.4 us: strip_program(): pl.pallas_call(functools.partial(round_kernel, first, last, n_frame, n_ro...]
    all_to_all x0 -> x2, blocking collectives: none -> 75.6 us  [the longest x1 56.1 us: strip_program(): got = lax.all_to_all(packed, BOTH, 0, 0, tiled=True)]
    reduce_sum x3 -> x0, other arithmetic: 29.1 us -> none  [shards(): total = jnp.sum(weight, axis=0)]
    add x18 -> x0, other arithmetic: 23.9 us -> none  [the longest x15 19.8 us: row_sum(): total = total + field[..., offset:offset + length, :]]
    another operation x3 -> x0, other arithmetic: 23.9 us -> none  [shards(): stacked = with_halo(jnp.stack((slope, offset_term)), (('row', 2),), 4)]
    ppermute x14 -> x6, starting transfers between devices: 30.4 us -> 16.3 us  [swap(): return (lax.ppermute(to_right, BOTH, up), lax.ppermute(to_left, BOTH, down))]
    ppermute x14 -> x6, waiting for transfers between devices: 19.1 us -> 7.94 us  [swap(): return (lax.ppermute(to_right, BOTH, up), lax.ppermute(to_left, BOTH, down))]
  transfers between devices with their start and end apart: 18 -> 6, of which waited for: 11 -> 3; matrix products, arithmetic and copies ran while one was open for 0% -> 0% of each run, Pallas kernels for 0% -> 0%
where the time goes in v2:
time: 225 us
  Pallas kernels  122 us (54%)
  blocking collectives  75.6 us (34%)
  starting transfers between devices  16.3 us (7%)
  waiting for transfers between devices  7.94 us (4%)
  local copies, waits for them, and re-layouts  2.49 us (1%)
    pallas_call x3, Pallas kernels, strip_program(): pl.pallas_call(functools.partial(round_kernel, first, last, n_frame, n_ro...  81.4 us
    all_to_all x1, blocking collectives, strip_program(): got = lax.all_to_all(packed, BOTH, 0, 0, tiled=True)  56.1 us
    pallas_call x1, Pallas kernels, strip_program(): pl.pallas_call(functools.partial(stats_kernel, width, strip), out_shape=(...  22.8 us
    all_to_all x1, blocking collectives, strip_program(): lax.all_to_all(result.reshape(n_dev, half, LANES), BOTH, 0, 0, tiled=True)  19.5 us
    ppermute x6, starting transfers between devices, swap(): return (lax.ppermute(to_right, BOTH, up), lax.ppermute(to_left, BOTH, down))  16.3 us
    pallas_call x1, Pallas kernels, strip_program(): pl.pallas_call(functools.partial(pack_kernel, rows), grid=(width // LANES...  10 us
    ppermute x6, waiting for transfers between devices, swap(): return (lax.ppermute(to_right, BOTH, up), lax.ppermute(to_left, BOTH, down))  7.94 us
    pallas_call x1, Pallas kernels, strip_program(): pl.pallas_call(functools.partial(unpack_kernel, rows), out_shape=(array(d...  6.27 us
  transfers between devices with their start and end apart: 6, of which 3 were waited for; matrix products, arithmetic and copies ran while one was open for 0% of the time, Pallas kernels for 0%

profile of v2, /device:TPU:0, one launch (start us, length us, event | category | flops | bytes accessed | tf_op | source)
XLA Modules:
  0.0 224.7 jit_solution(16396239855232056500)
XLA Ops:
  0.0 10.0 %pack.1 = f32[32,16,8,128]{3,2,1,0:T(8,128)} custom-call(f32[256,2048]{1,0:T(8,128)} %bitcast.4), custom_call_target="tpu_custom_call" | custom-call | tf_op jit(solution)/shard_map/pack/pallas_call | solution.py:274
  10.0 56.1 %all_to_all.10 = f32[32,16,8,128]{3,2,1,0:T(8,128)} all-to-all(f32[32,16,8,128]{3,2,1,0:T(8,128)} %pack.1), channel_id=1, replica_groups=mesh['frame'=8,'row'=4] {'frame','row'}, dimensions={0} | all-to-all | bytes 4194304 | tf_op jit(solution)/shard_map/all_to_all | solution.py:284
  66.1 6.3 %unpack.1 = (f32[64,64,128]{2,1,0:T(8,128)}, f32[64,8,128]{2,1,0:T(8,128)}, f32[64,8,128]{2,1,0:T(8,128)}) custom-call(f32[8,4,16,8,128]{4,3,2,1,0:T(8,128)} %bitcast.3), custom_call_target="tpu_custom_call" | custom-call | tf_op jit(solution)/shard_map/unpack/pallas_call | solution.py:287
  72.4 1.3 collective-permute-start
  73.7 1.3 collective-permute-start.1
  75.0 0.0 collective-permute-done.before_ref
  75.0 0.0 copy-start
  75.0 4.0 %collective-permute-done.1.after_ref = f32[64,8,128]{2,1,0:T(8,128)S(1)} collective-permute-done((f32[64,8,128]{2,1,0:T(8,128)}, f32[64,8,128]{2,1,0:T(8,128)S(1)}, u32[]{:S(2)}, u32[]{:S(2)}) %collective-permute-start.1) | collective-permute-done | bytes 262176 | tf_op jit(solution)/shard_map/ppermute | solution.py:297
  79.0 0.0 copy-start.1
  79.1 0.0 copy-done
  79.1 0.7 copy-done.1
  79.8 22.8 %stats.1 = (f32[80,80,128]{2,1,0:T(8,128)}, f32[72,72,128]{2,1,0:T(8,128)}, f32[72,72,128]{2,1,0:T(8,128)}, f32[80,80,128]{2,1,0:T(8,128)}) custom-call(f32[64,64,128]{2,1,0:T(8,128)} %get-tuple-element.18.s_ref, f32[64,8,128]{2,1,0:T(8,128)} %copy-done, f32[64,8,128]{2,1,0:T(8,128)} %copy-done.1), custom_call_target="tpu_custom_call" | custom-call | tf_op jit(solution)/shard_map/stats/pallas_call | solution.py:302
  102.6 0.6 broadcast_in_dim.3.refs_1_.refs_2_
  103.2 20.3 %round.3 = (f32[64,64,128]{2,1,0:T(8,128)}, f32[8,128]{1,0:T(8,128)}, f32[8,128]{1,0:T(8,128)}) custom-call(f32[80,80,128]{2,1,0:T(8,128)} %get-tuple-element.21.refs_0_, f32[8,128]{1,0:T(8,128)} %broadcast_in_dim.3.refs_1_.refs_2_, f32[8,128]{1,0:T(8,128)} %broadcast_in_dim.3.refs_1_.refs_2_, f32[80,80,128]{2,1,0:T(8,128)} %get-tuple-element.22.refs_3_, ...), custom_call_target="tpu_custom_call" | custom-call | tf_op jit(solution)/shard_map/round/pallas_call | solution.py:318
  123.4 6.7 %collective-permute-start.2 = (f32[8,128]{1,0:T(8,128)}, f32[8,128]{1,0:T(8,128)S(1)}, u32[]{:S(2)}, u32[]{:S(2)}) collective-permute-start(f32[8,128]{1,0:T(8,128)} %get-tuple-element.26), channel_id=1, source_target_pairs={{0,1},{1,2},{2,3},{3,4},{4,5},{5,6},{6,7},{7,8},{8,9},{9,10},{10,1... | collective-permute-start | bytes 12296 | tf_op jit(solution)/shard_map/ppermute | solution.py:297
  130.1 1.3 collective-permute-start.3
  131.4 0.0 collective-permute-done.2.refs_1_
  131.4 0.0 copy-start.2
  131.4 1.9 collective-permute-done.3.refs_2_
  133.4 0.0 copy-done.2
  133.4 0.6 copy-done.4
  134.0 30.8 %round.4 = (f32[64,64,128]{2,1,0:T(8,128)}, f32[8,128]{1,0:T(8,128)}, f32[8,128]{1,0:T(8,128)}) custom-call(f32[64,64,128]{2,1,0:T(8,128)} %get-tuple-element.25.refs_0_, f32[8,128]{1,0:T(8,128)} %copy-done.2, f32[8,128]{1,0:T(8,128)} %copy-done.4, f32[80,80,128]{2,1,0:T(8,128)} %get-tuple-element.22.refs_3_, f32[72,72,128]{2,1,0:T(8,128)} %get-tuple-element.23.refs_4_, ...), custom_call_target="tpu_custom_call" | custom-call | tf_op jit(solution)/shard_map/round/pallas_call | solution.py:318
  164.8 4.5 %collective-permute-start.4 = (f32[8,128]{1,0:T(8,128)}, f32[8,128]{1,0:T(8,128)S(1)}, u32[]{:S(2)}, u32[]{:S(2)}) collective-permute-start(f32[8,128]{1,0:T(8,128)} %get-tuple-element.29), channel_id=1, source_target_pairs={{0,1},{1,2},{2,3},{3,4},{4,5},{5,6},{6,7},{7,8},{8,9},{9,10},{10,1... | collective-permute-start | bytes 12296 | tf_op jit(solution)/shard_map/ppermute | solution.py:297
  169.3 1.3 collective-permute-start.5
  170.6 0.0 collective-permute-done.4.refs_1_
  170.6 0.0 copy-start.3
  170.6 1.9 collective-permute-done.5.refs_2_
  172.5 0.0 copy-done.3
  172.5 0.6 copy-done.5
  173.1 30.3 %round.5 = f32[8,4,16,128]{3,2,1,0:T(8,128)} custom-call(f32[64,64,128]{2,1,0:T(8,128)} %get-tuple-element.28.refs_0_, f32[8,128]{1,0:T(8,128)} %copy-done.3, f32[8,128]{1,0:T(8,128)} %copy-done.5, f32[80,80,128]{2,1,0:T(8,128)} %get-tuple-element.22.refs_3_, f32[72,72,128]{2,1,0:T(8,128)} %get-tuple-element.23.refs_4_, f32[72,72,128]{2,1,0:T(8,128)} %get-tuple-element.24.refs_5_), custom_call_target="tpu_custom_call" | custom-call | tf_op jit(solution)/shard_map/round/pallas_call | solution.py:318
  203.4 19.5 %all_to_all.11.r_ref = f32[32,16,128]{2,1,0:T(8,128)} all-to-all(f32[32,16,128]{2,1,0:T(8,128)} %bitcast.5), channel_id=1, replica_groups=mesh['frame'=8,'row'=4] {'frame','row'}, dimensions={0} | all-to-all | bytes 524288 | tf_op jit(solution)/shard_map/all_to_all | solution.py:330
  222.9 1.8 rows.1
  (2 shorter events, 0.0 us)
Async XLA Ops:
  72.4 2.6 %collective-permute-start = (f32[64,8,128]{2,1,0:T(8,128)}, f32[64,8,128]{2,1,0:T(8,128)S(1)}, u32[]{:S(2)}, u32[]{:S(2)}) collective-permute-start(f32[64,8,128]{2,1,0:T(8,128)} %get-tuple-element.19), channel_id=1, source_target_pairs={{0,1},{1,2},{2,3},{3,4},{4,5},{5,6},{6,7},{7,8},{8,9},{9,10},{10,1... | collective-permute-start | bytes 786440 | tf_op jit(solution)/shard_map/ppermute | solution.py:297
  73.7 5.3 %collective-permute-start.1 = (f32[64,8,128]{2,1,0:T(8,128)}, f32[64,8,128]{2,1,0:T(8,128)S(1)}, u32[]{:S(2)}, u32[]{:S(2)}) collective-permute-start(f32[64,8,128]{2,1,0:T(8,128)} %get-tuple-element.20), channel_id=1, source_target_pairs={{1,0},{2,1},{3,2},{4,3},{5,4},{6,5},{7,6},{8,7},{9,8},{10,9},{11,1... | collective-permute-start | bytes 786440 | tf_op jit(solution)/shard_map/ppermute | solution.py:297
  75.0 4.0 %copy-start = (f32[64,8,128]{2,1,0:T(8,128)}, f32[64,8,128]{2,1,0:T(8,128)S(1)}, u32[]{:S(2)}) copy-start(f32[64,8,128]{2,1,0:T(8,128)S(1)} %collective-permute-done.before_ref) | copy-start | bytes 786436
  79.0 0.7 copy-start.1
  123.4 8.0 %collective-permute-start.2 = (f32[8,128]{1,0:T(8,128)}, f32[8,128]{1,0:T(8,128)S(1)}, u32[]{:S(2)}, u32[]{:S(2)}) collective-permute-start(f32[8,128]{1,0:T(8,128)} %get-tuple-element.26), channel_id=1, source_target_pairs={{0,1},{1,2},{2,3},{3,4},{4,5},{5,6},{6,7},{7,8},{8,9},{9,10},{10,1... | collective-permute-start | bytes 12296 | tf_op jit(solution)/shard_map/ppermute | solution.py:297
  130.1 3.3 %collective-permute-start.3 = (f32[8,128]{1,0:T(8,128)}, f32[8,128]{1,0:T(8,128)S(1)}, u32[]{:S(2)}, u32[]{:S(2)}) collective-permute-start(f32[8,128]{1,0:T(8,128)} %get-tuple-element.27), channel_id=1, source_target_pairs={{1,0},{2,1},{3,2},{4,3},{5,4},{6,5},{7,6},{8,7},{9,8},{10,9},{11,1... | collective-permute-start | bytes 12296 | tf_op jit(solution)/shard_map/ppermute | solution.py:297
  131.4 2.0 copy-start.2
  133.4 0.6 copy-start.4
  164.8 5.8 %collective-permute-start.4 = (f32[8,128]{1,0:T(8,128)}, f32[8,128]{1,0:T(8,128)S(1)}, u32[]{:S(2)}, u32[]{:S(2)}) collective-permute-start(f32[8,128]{1,0:T(8,128)} %get-tuple-element.29), channel_id=1, source_target_pairs={{0,1},{1,2},{2,3},{3,4},{4,5},{5,6},{6,7},{7,8},{8,9},{9,10},{10,1... | collective-permute-start | bytes 12296 | tf_op jit(solution)/shard_map/ppermute | solution.py:297
  169.3 3.3 %collective-permute-start.5 = (f32[8,128]{1,0:T(8,128)}, f32[8,128]{1,0:T(8,128)S(1)}, u32[]{:S(2)}, u32[]{:S(2)}) collective-permute-start(f32[8,128]{1,0:T(8,128)} %get-tuple-element.30), channel_id=1, source_target_pairs={{1,0},{2,1},{3,2},{4,3},{5,4},{6,5},{7,6},{8,7},{9,8},{10,9},{11,1... | collective-permute-start | bytes 12296 | tf_op jit(solution)/shard_map/ppermute | solution.py:297
  170.6 2.0 copy-start.3
  172.5 0.6 copy-start.5

commit v3 on v2

--- a/solution.py
+++ b/solution.py
@@ -82,13 +82,15 @@
 def pack_kernel(rows, x_ref, out_ref, tmp):
     half = rows // 2
     low = lane_ids((GROUP, LANES)) < HALF
-    for f in range(GROUP):
-        tmp[f * (rows + 1) : f * (rows + 1) + rows] = x_ref[f * rows : (f + 1) * rows, :]
-    for i in range(half):
-        a = tmp[pl.ds(i, GROUP, stride=rows + 1), :]
-        b = tmp[pl.ds(i + half, GROUP, stride=rows + 1), :]
-        out_ref[0, i] = jnp.where(low, a, roll(b, HALF))
-        out_ref[1, i] = jnp.where(low, roll(a, HALF), b)
+    for k in range(x_ref.shape[1] // LANES):
+        here = slice(k * LANES, (k + 1) * LANES)
+        for f in range(GROUP):
+            tmp[k, f * (rows + 1) : f * (rows + 1) + rows] = x_ref[f * rows : (f + 1) * rows, here]
+        for i in range(half):
+            a = tmp[k, pl.ds(i, GROUP, stride=rows + 1), :]
+            b = tmp[k, pl.ds(i + half, GROUP, stride=rows + 1), :]
+            out_ref[2 * k, i] = jnp.where(low, a, roll(b, HALF))
+            out_ref[2 * k + 1, i] = jnp.where(low, roll(a, HALF), b)
 
 
 def unpack_kernel(rows, r_ref, s_ref, left_ref, right_ref):
@@ -107,27 +109,27 @@
         loop(half, 1, go)
 
 
-def stats_kernel(
-    width, strip, s_ref, before_ref, after_ref, full_ref, mean_ref, area_ref, est_ref, boxed, tmp
-):
+def prepare(width, strip, s_ref, before_ref, after_ref, full_ref, mean_ref, area_ref, est, boxed, tmp):
     rows, cols = s_ref.shape[0:2]
     wide = cols + HALO
     height = 2 * rows
     first_col = strip() * cols - RADIUS
     ones = halves_matrix()
 
-    def place(q):
-        full_ref[q + HALO, 0:HALO] = before_ref[q]
-        full_ref[q + HALO, HALO : HALO + cols] = s_ref[q]
-        full_ref[q + HALO, HALO + cols :] = after_ref[q]
-
-    loop(rows, 1, place)
+    def place(q0):
+        for q in (q0, q0 + 1, q0 + 2, q0 + 3):
+            full_ref[q + HALO, 0:HALO] = before_ref[q]
+            full_ref[q + HALO, HALO : HALO + cols] = s_ref[q]
+            full_ref[q + HALO, HALO + cols :] = after_ref[q]
+
+    loop(rows, 4, place)
     row_halo(full_ref, rows)
 
     def first(q):
-        est_ref[q] = frame_sum(full_ref[q], ones) / HALF
-
-    loop(rows + 2 * HALO, 1, first)
+        v = full_ref[pl.ds(q, 4)]
+        est[pl.ds(q, 4)] = (frame_sum(v.reshape(-1, LANES), ones) / HALF).reshape(v.shape)
+
+    loop(rows + 2 * HALO, 4, first)
 
     step = rows // 8 * 3
 
@@ -138,40 +140,57 @@
     loop(rows + HALO, step, down)
 
     col = first_col + lax.broadcasted_iota(jnp.int32, (wide, LANES), 0)
-    upper = jnp.where(lane_ids((wide, LANES)) < HALF, 0, rows)
+    upper = jnp.where(lane_ids((8, LANES)) < HALF, 0, rows)
     col_inverse = jnp.where(
         jnp.logical_and(col >= 0, col < width), 1.0 / count(col, width), 0.0
     )
 
-    def means(q):
-        row = q - RADIUS + upper
-        inside = jnp.logical_and(row >= 0, row < height)
-        area = jnp.where(inside, col_inverse / count(row, height), 0.0)
-        area_ref[q] = area
-        mean_ref[q] = col_box(boxed, q, tmp) * area
-
-    loop(rows + HALO, 1, means)
-
-
-def round_kernel(first, last, n_frame, n_row, *refs):
-    e_ref, before_ref, after_ref, s_ref, mean_ref, area_ref = refs[0:6]
-    outs, scratch = (refs[6:7], refs[7:]) if last else (refs[6:9], refs[9:])
-    ext, b1, b2, b3, slope, offset, tmp, flat = scratch
+    def means(q0):
+        for k in range(4):
+            q = q0 + k
+            row = q - RADIUS + upper
+            inside = jnp.logical_and(row >= 0, row < height)
+            row_inverse = jnp.where(inside, 1.0 / count(row, height), 0.0)
+            area = col_inverse * jnp.concatenate([row_inverse] * (wide // 8), axis=0)
+            area_ref[q] = area
+            mean_ref[q] = col_box(boxed, q, tmp.at[k]) * area
+
+    loop(rows + HALO, 4, means)
+
+
+def round_kernel(first, last, width, strip, n_frame, n_row, *refs):
+    if first:
+        centre_ref, before_ref, after_ref = refs[0:3]
+        outs, (s_ref, mean_ref, area_ref), scratch = refs[3:6], refs[6:9], refs[9:]
+    else:
+        e_ref, before_ref, after_ref, s_ref, mean_ref, area_ref = refs[0:6]
+        outs, scratch = (refs[6:7], refs[7:]) if last else (refs[6:9], refs[9:])
+    est, b1, b2, b3, slope, offset, tmp, w_buf, t_buf, flat = scratch
     rows = mean_ref.shape[0] - HALO
     cols = mean_ref.shape[1] - HALO
     ones = halves_matrix()
-    est = e_ref if first else ext
     edge_row = lane_ids((HALO, LANES)) % HALF
 
-    if not first:
-        def place(q):
-            here = edge_row == q
-            ext[q + HALO, 0:HALO] = frame_sum(jnp.where(here, before_ref[...], 0.0), ones)
-            ext[q + HALO, HALO : HALO + cols] = e_ref[q]
-            ext[q + HALO, HALO + cols :] = frame_sum(jnp.where(here, after_ref[...], 0.0), ones)
-
-        loop(rows, 1, place)
-        row_halo(ext, rows)
+    if first:
+        prepare(
+            width, strip, centre_ref, before_ref, after_ref, s_ref, mean_ref, area_ref, est, b1, tmp
+        )
+    else:
+        def place(q0):
+            edges = [
+                jnp.where(edge_row == q0 + k, ref[...], 0.0)
+                for ref in (before_ref, after_ref)
+                for k in range(8)
+            ]
+            v = frame_sum(jnp.concatenate(edges, axis=0), ones)
+            for k in range(8):
+                q = q0 + k
+                est[q + HALO, 0:HALO] = v[HALO * k : HALO * (k + 1)]
+                est[q + HALO, HALO : HALO + cols] = e_ref[q]
+                est[q + HALO, HALO + cols :] = v[HALO * (8 + k) : HALO * (9 + k)]
+
+        loop(rows, 8, place)
+        row_halo(est, rows)
 
     step = rows // 8 * 3
 
@@ -218,21 +237,37 @@
             b = col_box(b2.at[:, 0 : cols + HALO], q, tmp.at[2 * k + 1])
             gap = ((a * e + b) * area - e) * (1.0 / CAUCHY_SCALE)
             weight = 1.0 / (1.0 + gap * gap)
-            new = frame_sum(weight * p, ones) / frame_sum(weight, ones)
-            if last:
-                flat[...] = jnp.where(lane == q, new, flat[...])
-            else:
-                outs[0][q] = new
-                here = edge_row == q
-                outs[1][...] = jnp.where(here, new[0:HALO], outs[1][...])
-                outs[2][...] = jnp.where(here, new[cols - HALO :], outs[2][...])
+            w_buf[q] = weight * p
+            t_buf[q] = weight
+
+    loop(rows, 2, weigh)
 
     if last:
         flat[...] = jnp.zeros_like(flat)
     else:
         outs[1][...] = jnp.zeros_like(outs[1])
         outs[2][...] = jnp.zeros_like(outs[2])
-    loop(rows, 2, weigh)
+
+    def merge(q0):
+        w = frame_sum(w_buf[pl.ds(q0, 4)].reshape(4 * cols, LANES), ones)
+        t = frame_sum(t_buf[pl.ds(q0, 4)].reshape(4 * cols, LANES), ones)
+        new = (w / t).reshape(4, cols, LANES)
+        if last:
+            v = flat[...]
+            for k in range(4):
+                v = jnp.where(lane == q0 + k, new[k], v)
+            flat[...] = v
+        else:
+            outs[0][pl.ds(q0, 4)] = new
+            left, right = outs[1][...], outs[2][...]
+            for k in range(4):
+                here = edge_row == q0 + k
+                left = jnp.where(here, new[k, 0:HALO], left)
+                right = jnp.where(here, new[k, cols - HALO :], right)
+            outs[1][...] = left
+            outs[2][...] = right
+
+    loop(rows, 4, merge)
 
     if last:
         shard = 2 * rows // n_row
@@ -273,11 +308,11 @@
 
     packed = pl.pallas_call(
         functools.partial(pack_kernel, rows),
-        grid=(width // LANES,),
-        in_specs=[pl.BlockSpec((local * rows, LANES), lambda k: (0, k))],
-        out_specs=pl.BlockSpec((2, half, GROUP, LANES), lambda k: (k, 0, 0, 0)),
+        grid=(4,),
+        in_specs=[pl.BlockSpec((local * rows, width // 4), lambda k: (0, k))],
+        out_specs=pl.BlockSpec((n_dev // 4, half, GROUP, LANES), lambda k: (k, 0, 0, 0)),
         out_shape=array(n_dev, half, GROUP),
-        scratch_shapes=[scratch(GROUP * (rows + 1))],
+        scratch_shapes=[scratch(width // 4 // LANES, GROUP * (rows + 1))],
         name="pack",
     )(frames.reshape(local * rows, width))
 
@@ -299,32 +334,30 @@
     before, after = swap(left_edge, right_edge)
     whole = (deep + 2 * HALO, cols + 2 * HALO)
     fitted = (deep + HALO, cols + HALO)
-    full, mean, area, est = pl.pallas_call(
-        functools.partial(stats_kernel, width, strip),
-        out_shape=(array(*whole), array(*fitted), array(*fitted), array(*whole)),
-        scratch_shapes=[scratch(fitted[0], whole[1]), scratch(whole[1])],
-        name="stats",
-    )(centre, before, after)
-
-    before = after = jnp.zeros((HALO, LANES), f32)
-    for k in range(ROUNDS):
+    work = [scratch(*whole)] + [scratch(fitted[0], whole[1])] * 3 + [scratch(*fitted)] * 2
+    work += [scratch(6, whole[1]), scratch(deep, cols), scratch(deep, cols), scratch(cols)]
+    estimate_out = (array(deep, cols), array(HALO), array(HALO))
+
+    def run_round(k, *operands):
         first, last = k == 0, k == ROUNDS - 1
-        if not first:
-            before, after = swap(left_edge, right_edge)
         if last:
             out_shape = array(n_frame, n_row, half)
+        elif first:
+            out_shape = estimate_out + (array(*whole), array(*fitted), array(*fitted))
         else:
-            out_shape = (array(deep, cols), array(HALO), array(HALO))
-        result = pl.pallas_call(
-            functools.partial(round_kernel, first, last, n_frame, n_row),
+            out_shape = estimate_out
+        return pl.pallas_call(
+            functools.partial(round_kernel, first, last, width, strip, n_frame, n_row),
             out_shape=out_shape,
-            scratch_shapes=[scratch(*whole)]
-            + [scratch(fitted[0], whole[1])] * 3
-            + [scratch(*fitted)] * 2
-            + [scratch(6, whole[1]), scratch(cols)],
+            scratch_shapes=work,
             name="round",
-        )(est, before, after, full, mean, area)
-        if not last:
+        )(*operands)
+
+    est, left_edge, right_edge, *fixed = run_round(0, centre, before, after)
+    for k in range(1, ROUNDS):
+        before, after = swap(left_edge, right_edge)
+        result = run_round(k, est, before, after, *fixed)
+        if k < ROUNDS - 1:
             est, left_edge, right_edge = result
 
     got = lax.all_to_all(result.reshape(n_dev, half, LANES), BOTH, 0, 0, tiled=True)

time: 225 us -> 177 us (0.79)
  Pallas kernels: 122 us -> 74.5 us
    pallas_call x5 -> x4, Pallas kernels: 114 us -> 66.4 us  [the longest x3 62.3 us: run_round(): pl.pallas_call(functools.partial(round_kernel, first, last, width, strip,...]
where the time goes in v3:
time: 177 us; the launch traced here: 176 us
  blocking collectives  75.6 us (43%)
  Pallas kernels  74.5 us (42%)
  starting transfers between devices  16.3 us (9%)
  waiting for transfers between devices  7.94 us (4%)
  local copies, waits for them, and re-layouts  1.89 us (1%)
    pallas_call x3, Pallas kernels, run_round(): pl.pallas_call(functools.partial(round_kernel, first, last, width, strip,...  62.3 us
    all_to_all x1, blocking collectives, strip_program(): got = lax.all_to_all(packed, BOTH, 0, 0, tiled=True)  56.1 us
    all_to_all x1, blocking collectives, strip_program(): lax.all_to_all(result.reshape(n_dev, half, LANES), BOTH, 0, 0, tiled=True)  19.5 us
    ppermute x6, starting transfers between devices, swap(): return (lax.ppermute(to_right, BOTH, up), lax.ppermute(to_left, BOTH, down))  16.3 us
    ppermute x6, waiting for transfers between devices, swap(): return (lax.ppermute(to_right, BOTH, up), lax.ppermute(to_left, BOTH, down))  7.94 us
    pallas_call x1, Pallas kernels, strip_program(): pl.pallas_call(functools.partial(unpack_kernel, rows), out_shape=(array(d...  6.26 us
    pallas_call x1, Pallas kernels, strip_program(): pl.pallas_call(functools.partial(pack_kernel, rows), grid=(4,), in_specs=...  4.16 us
  transfers between devices with their start and end apart: 6, of which 3 were waited for; matrix products, arithmetic and copies ran while one was open for 0% of the time, Pallas kernels for 0%

profile of v3, /device:TPU:0, one launch (start us, length us, event | category | flops | bytes accessed | tf_op | source)
XLA Modules:
  0.0 176.3 jit_solution(17745518963573888152)
XLA Ops:
  0.0 4.2 %pack.1 = f32[32,16,8,128]{3,2,1,0:T(8,128)} custom-call(f32[256,2048]{1,0:T(8,128)} %bitcast.4), custom_call_target="tpu_custom_call" | custom-call | tf_op jit(solution)/shard_map/pack/pallas_call | solution.py:309
  4.2 56.1 %all_to_all.10 = f32[32,16,8,128]{3,2,1,0:T(8,128)} all-to-all(f32[32,16,8,128]{3,2,1,0:T(8,128)} %pack.1), channel_id=1, replica_groups=mesh['frame'=8,'row'=4] {'frame','row'}, dimensions={0} | all-to-all | bytes 4194304 | tf_op jit(solution)/shard_map/all_to_all | solution.py:319
  60.3 6.3 %unpack.1 = (f32[64,64,128]{2,1,0:T(8,128)}, f32[64,8,128]{2,1,0:T(8,128)}, f32[64,8,128]{2,1,0:T(8,128)}) custom-call(f32[8,4,16,8,128]{4,3,2,1,0:T(8,128)} %bitcast.3), custom_call_target="tpu_custom_call" | custom-call | tf_op jit(solution)/shard_map/unpack/pallas_call | solution.py:322
  66.5 1.3 collective-permute-start
  67.8 1.3 collective-permute-start.1
  69.1 0.0 collective-permute-done.refs_1_
  69.2 0.0 copy-start
  69.2 4.0 %collective-permute-done.1.refs_2_ = f32[64,8,128]{2,1,0:T(8,128)S(1)} collective-permute-done((f32[64,8,128]{2,1,0:T(8,128)}, f32[64,8,128]{2,1,0:T(8,128)S(1)}, u32[]{:S(2)}, u32[]{:S(2)}) %collective-permute-start.1) | collective-permute-done | bytes 262176 | tf_op jit(solution)/shard_map/ppermute | solution.py:332
  73.2 0.0 copy-start.1
  73.2 0.0 copy-done
  73.2 0.7 copy-done.1
  73.9 24.0 %round.3 = (f32[64,64,128]{2,1,0:T(8,128)}, f32[8,128]{1,0:T(8,128)}, f32[8,128]{1,0:T(8,128)}, f32[80,80,128]{2,1,0:T(8,128)}, f32[72,72,128]{2,1,0:T(8,128)}, /*index=5*/f32[72,72,128]{2,1,0:T(8,128)}) custom-call(f32[64,64,128]{2,1,0:T(8,128)} %get-tuple-element.17.refs_0_, f32[64,8,128]{2,1,0:T(8,128)} %copy-done, f32[64,8,128]{2,1,0:T(8,128)} %copy-done.1), custom_call_target="tpu_custom_call" | custom-call | tf_op jit(solution)/shard_map/round/pallas_call | solution.py:349
  97.9 6.6 %collective-permute-start.2 = (f32[8,128]{1,0:T(8,128)}, f32[8,128]{1,0:T(8,128)S(1)}, u32[]{:S(2)}, u32[]{:S(2)}) collective-permute-start(f32[8,128]{1,0:T(8,128)} %get-tuple-element.21), channel_id=1, source_target_pairs={{0,1},{1,2},{2,3},{3,4},{4,5},{5,6},{6,7},{7,8},{8,9},{9,10},{10,1... | collective-permute-start | bytes 12296 | tf_op jit(solution)/shard_map/ppermute | solution.py:332
  104.6 1.3 collective-permute-start.3
  105.9 0.0 collective-permute-done.2.refs_1_
  105.9 0.0 copy-start.2
  105.9 1.9 %collective-permute-done.3.refs_2_ = f32[8,128]{1,0:T(8,128)S(1)} collective-permute-done((f32[8,128]{1,0:T(8,128)}, f32[8,128]{1,0:T(8,128)S(1)}, u32[]{:S(2)}, u32[]{:S(2)}) %collective-permute-start.3) | collective-permute-done | bytes 4128 | tf_op jit(solution)/shard_map/ppermute | solution.py:332
  107.8 0.0 copy-start.4
  107.8 0.0 copy-done.2
  107.8 0.6 copy-done.4
  108.4 19.4 %round.4 = (f32[64,64,128]{2,1,0:T(8,128)}, f32[8,128]{1,0:T(8,128)}, f32[8,128]{1,0:T(8,128)}) custom-call(f32[64,64,128]{2,1,0:T(8,128)} %get-tuple-element.20.refs_0_, f32[8,128]{1,0:T(8,128)} %copy-done.2, f32[8,128]{1,0:T(8,128)} %copy-done.4, f32[80,80,128]{2,1,0:T(8,128)} %get-tuple-element.23.refs_3_, f32[72,72,128]{2,1,0:T(8,128)} %get-tuple-element.24.refs_4_, ...), custom_call_target="tpu_custom_call" | custom-call | tf_op jit(solution)/shard_map/round/pallas_call | solution.py:349
  127.8 4.5 %collective-permute-start.4 = (f32[8,128]{1,0:T(8,128)}, f32[8,128]{1,0:T(8,128)S(1)}, u32[]{:S(2)}, u32[]{:S(2)}) collective-permute-start(f32[8,128]{1,0:T(8,128)} %get-tuple-element.27), channel_id=1, source_target_pairs={{0,1},{1,2},{2,3},{3,4},{4,5},{5,6},{6,7},{7,8},{8,9},{9,10},{10,1... | collective-permute-start | bytes 12296 | tf_op jit(solution)/shard_map/ppermute | solution.py:332
  132.3 1.3 collective-permute-start.5
  133.6 0.0 collective-permute-done.4.refs_1_
  133.6 0.0 copy-start.3
  133.6 1.9 %collective-permute-done.5.refs_2_ = f32[8,128]{1,0:T(8,128)S(1)} collective-permute-done((f32[8,128]{1,0:T(8,128)}, f32[8,128]{1,0:T(8,128)S(1)}, u32[]{:S(2)}, u32[]{:S(2)}) %collective-permute-start.5) | collective-permute-done | bytes 4128 | tf_op jit(solution)/shard_map/ppermute | solution.py:332
  135.6 0.0 copy-start.5
  135.6 0.0 copy-done.3
  135.6 0.6 copy-done.5
  136.1 18.9 %round.5 = f32[8,4,16,128]{3,2,1,0:T(8,128)} custom-call(f32[64,64,128]{2,1,0:T(8,128)} %get-tuple-element.26.refs_0_, f32[8,128]{1,0:T(8,128)} %copy-done.3, f32[8,128]{1,0:T(8,128)} %copy-done.5, f32[80,80,128]{2,1,0:T(8,128)} %get-tuple-element.23.refs_3_, f32[72,72,128]{2,1,0:T(8,128)} %get-tuple-element.24.refs_4_, f32[72,72,128]{2,1,0:T(8,128)} %get-tuple-element.25.refs_5_), custom_call_target="tpu_custom_call" | custom-call | tf_op jit(solution)/shard_map/round/pallas_call | solution.py:349
  155.0 19.5 %all_to_all.11.r_ref = f32[32,16,128]{2,1,0:T(8,128)} all-to-all(f32[32,16,128]{2,1,0:T(8,128)} %bitcast.5), channel_id=1, replica_groups=mesh['frame'=8,'row'=4] {'frame','row'}, dimensions={0} | all-to-all | bytes 524288 | tf_op jit(solution)/shard_map/all_to_all | solution.py:363
  174.5 1.8 %rows.1 = f32[32,2048]{1,0:T(8,128)} custom-call(f32[32,16,128]{2,1,0:T(8,128)} %all_to_all.11.r_ref), custom_call_target="tpu_custom_call" | custom-call | tf_op jit(solution)/shard_map/rows/pallas_call | solution.py:364
Async XLA Ops:
  66.5 2.6 %collective-permute-start = (f32[64,8,128]{2,1,0:T(8,128)}, f32[64,8,128]{2,1,0:T(8,128)S(1)}, u32[]{:S(2)}, u32[]{:S(2)}) collective-permute-start(f32[64,8,128]{2,1,0:T(8,128)} %get-tuple-element.18), channel_id=1, source_target_pairs={{0,1},{1,2},{2,3},{3,4},{4,5},{5,6},{6,7},{7,8},{8,9},{9,10},{10,1... | collective-permute-start | bytes 786440 | tf_op jit(solution)/shard_map/ppermute | solution.py:332
  67.8 5.3 %collective-permute-start.1 = (f32[64,8,128]{2,1,0:T(8,128)}, f32[64,8,128]{2,1,0:T(8,128)S(1)}, u32[]{:S(2)}, u32[]{:S(2)}) collective-permute-start(f32[64,8,128]{2,1,0:T(8,128)} %get-tuple-element.19), channel_id=1, source_target_pairs={{1,0},{2,1},{3,2},{4,3},{5,4},{6,5},{7,6},{8,7},{9,8},{10,9},{11,1... | collective-permute-start | bytes 786440 | tf_op jit(solution)/shard_map/ppermute | solution.py:332
  69.2 4.0 %copy-start = (f32[64,8,128]{2,1,0:T(8,128)}, f32[64,8,128]{2,1,0:T(8,128)S(1)}, u32[]{:S(2)}) copy-start(f32[64,8,128]{2,1,0:T(8,128)S(1)} %collective-permute-done.refs_1_) | copy-start | bytes 786436
  73.2 0.7 copy-start.1
  97.9 8.0 %collective-permute-start.2 = (f32[8,128]{1,0:T(8,128)}, f32[8,128]{1,0:T(8,128)S(1)}, u32[]{:S(2)}, u32[]{:S(2)}) collective-permute-start(f32[8,128]{1,0:T(8,128)} %get-tuple-element.21), channel_id=1, source_target_pairs={{0,1},{1,2},{2,3},{3,4},{4,5},{5,6},{6,7},{7,8},{8,9},{9,10},{10,1... | collective-permute-start | bytes 12296 | tf_op jit(solution)/shard_map/ppermute | solution.py:332
  104.6 3.3 %collective-permute-start.3 = (f32[8,128]{1,0:T(8,128)}, f32[8,128]{1,0:T(8,128)S(1)}, u32[]{:S(2)}, u32[]{:S(2)}) collective-permute-start(f32[8,128]{1,0:T(8,128)} %get-tuple-element.22), channel_id=1, source_target_pairs={{1,0},{2,1},{3,2},{4,3},{5,4},{6,5},{7,6},{8,7},{9,8},{10,9},{11,1... | collective-permute-start | bytes 12296 | tf_op jit(solution)/shard_map/ppermute | solution.py:332
  105.9 2.0 %copy-start.2 = (f32[8,128]{1,0:T(8,128)}, f32[8,128]{1,0:T(8,128)S(1)}, u32[]{:S(2)}) copy-start(f32[8,128]{1,0:T(8,128)S(1)} %collective-permute-done.2.refs_1_) | copy-start | bytes 12292
  107.8 0.6 copy-start.4
  127.8 5.8 %collective-permute-start.4 = (f32[8,128]{1,0:T(8,128)}, f32[8,128]{1,0:T(8,128)S(1)}, u32[]{:S(2)}, u32[]{:S(2)}) collective-permute-start(f32[8,128]{1,0:T(8,128)} %get-tuple-element.27), channel_id=1, source_target_pairs={{0,1},{1,2},{2,3},{3,4},{4,5},{5,6},{6,7},{7,8},{8,9},{9,10},{10,1... | collective-permute-start | bytes 12296 | tf_op jit(solution)/shard_map/ppermute | solution.py:332
  132.3 3.3 %collective-permute-start.5 = (f32[8,128]{1,0:T(8,128)}, f32[8,128]{1,0:T(8,128)S(1)}, u32[]{:S(2)}, u32[]{:S(2)}) collective-permute-start(f32[8,128]{1,0:T(8,128)} %get-tuple-element.28), channel_id=1, source_target_pairs={{1,0},{2,1},{3,2},{4,3},{5,4},{6,5},{7,6},{8,7},{9,8},{10,9},{11,1... | collective-permute-start | bytes 12296 | tf_op jit(solution)/shard_map/ppermute | solution.py:332
  133.6 2.0 %copy-start.3 = (f32[8,128]{1,0:T(8,128)}, f32[8,128]{1,0:T(8,128)S(1)}, u32[]{:S(2)}) copy-start(f32[8,128]{1,0:T(8,128)S(1)} %collective-permute-done.4.refs_1_) | copy-start | bytes 12292
  135.6 0.6 copy-start.5

commit v4 on v3

--- a/solution.py
+++ b/solution.py
@@ -204,7 +204,7 @@
     loop(rows + HALO, step, down)
 
     def fit(q0):
-        for k in range(2):
+        for k in range(4):
             q = q0 + k
             area, mean = area_ref[q], mean_ref[q]
             guide = col_box(b2, q, tmp.at[3 * k]) * area
@@ -214,7 +214,7 @@
             slope[q] = a
             offset[q] = mean - a * guide
 
-    loop(rows + HALO, 2, fit)
+    loop(rows + HALO, 4, fit)
 
     block = rows // 4
 
@@ -228,7 +228,7 @@
     lane = edge_row[0:1]
 
     def weigh(q0):
-        for k in range(2):
+        for k in range(4):
             q = q0 + k
             area = area_ref[q + RADIUS, RADIUS : RADIUS + cols]
             e = est[q + HALO, HALO : HALO + cols]
@@ -240,7 +240,7 @@
             w_buf[q] = weight * p
             t_buf[q] = weight
 
-    loop(rows, 2, weigh)
+    loop(rows, 4, weigh)
 
     if last:
         flat[...] = jnp.zeros_like(flat)
@@ -335,7 +335,7 @@
     whole = (deep + 2 * HALO, cols + 2 * HALO)
     fitted = (deep + HALO, cols + HALO)
     work = [scratch(*whole)] + [scratch(fitted[0], whole[1])] * 3 + [scratch(*fitted)] * 2
-    work += [scratch(6, whole[1]), scratch(deep, cols), scratch(deep, cols), scratch(cols)]
+    work += [scratch(12, whole[1]), scratch(deep, cols), scratch(deep, cols), scratch(cols)]
     estimate_out = (array(deep, cols), array(HALO), array(HALO))
 
     def run_round(k, *operands):

time: 177 us -> 175 us (0.989)
  no operation moved by 1% of the time
where the time goes in v4:
time: 175 us
  blocking collectives  75.6 us (43%)
  Pallas kernels  73.2 us (42%)
  starting transfers between devices  16.3 us (9%)
  waiting for transfers between devices  7.94 us (5%)
  local copies, waits for them, and re-layouts  1.89 us (1%)
    pallas_call x3, Pallas kernels, run_round(): pl.pallas_call(functools.partial(round_kernel, first, last, width, strip,...  61 us
    all_to_all x1, blocking collectives, strip_program(): got = lax.all_to_all(packed, BOTH, 0, 0, tiled=True)  56.1 us
    all_to_all x1, blocking collectives, strip_program(): lax.all_to_all(result.reshape(n_dev, half, LANES), BOTH, 0, 0, tiled=True)  19.5 us
    ppermute x6, starting transfers between devices, swap(): return (lax.ppermute(to_right, BOTH, up), lax.ppermute(to_left, BOTH, down))  16.3 us
    ppermute x6, waiting for transfers between devices, swap(): return (lax.ppermute(to_right, BOTH, up), lax.ppermute(to_left, BOTH, down))  7.94 us
    pallas_call x1, Pallas kernels, strip_program(): pl.pallas_call(functools.partial(unpack_kernel, rows), out_shape=(array(d...  6.26 us
    pallas_call x1, Pallas kernels, strip_program(): pl.pallas_call(functools.partial(pack_kernel, rows), grid=(4,), in_specs=...  4.16 us
  transfers between devices with their start and end apart: 6, of which 3 were waited for; matrix products, arithmetic and copies ran while one was open for 0% of the time, Pallas kernels for 0%

profile of v4, /device:TPU:0, one launch (start us, length us, event | category | flops | bytes accessed | tf_op | source)
XLA Modules:
  0.0 175.0 jit_solution(5205899739537861699)
XLA Ops:
  0.0 4.2 %pack.1 = f32[32,16,8,128]{3,2,1,0:T(8,128)} custom-call(f32[256,2048]{1,0:T(8,128)} %bitcast.4), custom_call_target="tpu_custom_call" | custom-call | tf_op jit(solution)/shard_map/pack/pallas_call | solution.py:309
  4.2 56.1 %all_to_all.10 = f32[32,16,8,128]{3,2,1,0:T(8,128)} all-to-all(f32[32,16,8,128]{3,2,1,0:T(8,128)} %pack.1), channel_id=1, replica_groups=mesh['frame'=8,'row'=4] {'frame','row'}, dimensions={0} | all-to-all | bytes 4194304 | tf_op jit(solution)/shard_map/all_to_all | solution.py:319
  60.3 6.3 %unpack.1 = (f32[64,64,128]{2,1,0:T(8,128)}, f32[64,8,128]{2,1,0:T(8,128)}, f32[64,8,128]{2,1,0:T(8,128)}) custom-call(f32[8,4,16,8,128]{4,3,2,1,0:T(8,128)} %bitcast.3), custom_call_target="tpu_custom_call" | custom-call | tf_op jit(solution)/shard_map/unpack/pallas_call | solution.py:322
  66.5 1.3 collective-permute-start
  67.8 1.3 collective-permute-start.1
  69.1 0.0 collective-permute-done.refs_1_
  69.2 0.0 copy-start
  69.2 4.0 %collective-permute-done.1.refs_2_ = f32[64,8,128]{2,1,0:T(8,128)S(1)} collective-permute-done((f32[64,8,128]{2,1,0:T(8,128)}, f32[64,8,128]{2,1,0:T(8,128)S(1)}, u32[]{:S(2)}, u32[]{:S(2)}) %collective-permute-start.1) | collective-permute-done | bytes 262176 | tf_op jit(solution)/shard_map/ppermute | solution.py:332
  73.2 0.0 copy-start.1
  73.2 0.0 copy-done
  73.2 0.7 copy-done.1
  73.9 23.6 %round.3 = (f32[64,64,128]{2,1,0:T(8,128)}, f32[8,128]{1,0:T(8,128)}, f32[8,128]{1,0:T(8,128)}, f32[80,80,128]{2,1,0:T(8,128)}, f32[72,72,128]{2,1,0:T(8,128)}, /*index=5*/f32[72,72,128]{2,1,0:T(8,128)}) custom-call(f32[64,64,128]{2,1,0:T(8,128)} %get-tuple-element.17.refs_0_, f32[64,8,128]{2,1,0:T(8,128)} %copy-done, f32[64,8,128]{2,1,0:T(8,128)} %copy-done.1), custom_call_target="tpu_custom_call" | custom-call | tf_op jit(solution)/shard_map/round/pallas_call | solution.py:349
  97.5 6.6 %collective-permute-start.2 = (f32[8,128]{1,0:T(8,128)}, f32[8,128]{1,0:T(8,128)S(1)}, u32[]{:S(2)}, u32[]{:S(2)}) collective-permute-start(f32[8,128]{1,0:T(8,128)} %get-tuple-element.21), channel_id=1, source_target_pairs={{0,1},{1,2},{2,3},{3,4},{4,5},{5,6},{6,7},{7,8},{8,9},{9,10},{10,1... | collective-permute-start | bytes 12296 | tf_op jit(solution)/shard_map/ppermute | solution.py:332
  104.1 1.3 collective-permute-start.3
  105.4 0.0 collective-permute-done.2.refs_1_
  105.5 0.0 copy-start.2
  105.5 1.9 %collective-permute-done.3.refs_2_ = f32[8,128]{1,0:T(8,128)S(1)} collective-permute-done((f32[8,128]{1,0:T(8,128)}, f32[8,128]{1,0:T(8,128)S(1)}, u32[]{:S(2)}, u32[]{:S(2)}) %collective-permute-start.3) | collective-permute-done | bytes 4128 | tf_op jit(solution)/shard_map/ppermute | solution.py:332
  107.4 0.0 copy-start.4
  107.4 0.0 copy-done.2
  107.4 0.6 copy-done.4
  108.0 18.9 %round.4 = (f32[64,64,128]{2,1,0:T(8,128)}, f32[8,128]{1,0:T(8,128)}, f32[8,128]{1,0:T(8,128)}) custom-call(f32[64,64,128]{2,1,0:T(8,128)} %get-tuple-element.20.refs_0_, f32[8,128]{1,0:T(8,128)} %copy-done.2, f32[8,128]{1,0:T(8,128)} %copy-done.4, f32[80,80,128]{2,1,0:T(8,128)} %get-tuple-element.23.refs_3_, f32[72,72,128]{2,1,0:T(8,128)} %get-tuple-element.24.refs_4_, ...), custom_call_target="tpu_custom_call" | custom-call | tf_op jit(solution)/shard_map/round/pallas_call | solution.py:349
  126.9 4.5 %collective-permute-start.4 = (f32[8,128]{1,0:T(8,128)}, f32[8,128]{1,0:T(8,128)S(1)}, u32[]{:S(2)}, u32[]{:S(2)}) collective-permute-start(f32[8,128]{1,0:T(8,128)} %get-tuple-element.27), channel_id=1, source_target_pairs={{0,1},{1,2},{2,3},{3,4},{4,5},{5,6},{6,7},{7,8},{8,9},{9,10},{10,1... | collective-permute-start | bytes 12296 | tf_op jit(solution)/shard_map/ppermute | solution.py:332
  131.4 1.3 collective-permute-start.5
  132.7 0.0 collective-permute-done.4.refs_1_
  132.7 0.0 copy-start.3
  132.7 1.9 %collective-permute-done.5.refs_2_ = f32[8,128]{1,0:T(8,128)S(1)} collective-permute-done((f32[8,128]{1,0:T(8,128)}, f32[8,128]{1,0:T(8,128)S(1)}, u32[]{:S(2)}, u32[]{:S(2)}) %collective-permute-start.5) | collective-permute-done | bytes 4128 | tf_op jit(solution)/shard_map/ppermute | solution.py:332
  134.7 0.0 copy-start.5
  134.7 0.0 copy-done.3
  134.7 0.6 copy-done.5
  135.3 18.5 %round.5 = f32[8,4,16,128]{3,2,1,0:T(8,128)} custom-call(f32[64,64,128]{2,1,0:T(8,128)} %get-tuple-element.26.refs_0_, f32[8,128]{1,0:T(8,128)} %copy-done.3, f32[8,128]{1,0:T(8,128)} %copy-done.5, f32[80,80,128]{2,1,0:T(8,128)} %get-tuple-element.23.refs_3_, f32[72,72,128]{2,1,0:T(8,128)} %get-tuple-element.24.refs_4_, f32[72,72,128]{2,1,0:T(8,128)} %get-tuple-element.25.refs_5_), custom_call_target="tpu_custom_call" | custom-call | tf_op jit(solution)/shard_map/round/pallas_call | solution.py:349
  153.7 19.5 %all_to_all.11.r_ref = f32[32,16,128]{2,1,0:T(8,128)} all-to-all(f32[32,16,128]{2,1,0:T(8,128)} %bitcast.5), channel_id=1, replica_groups=mesh['frame'=8,'row'=4] {'frame','row'}, dimensions={0} | all-to-all | bytes 524288 | tf_op jit(solution)/shard_map/all_to_all | solution.py:363
  173.2 1.8 %rows.1 = f32[32,2048]{1,0:T(8,128)} custom-call(f32[32,16,128]{2,1,0:T(8,128)} %all_to_all.11.r_ref), custom_call_target="tpu_custom_call" | custom-call | tf_op jit(solution)/shard_map/rows/pallas_call | solution.py:364
Async XLA Ops:
  66.5 2.6 %collective-permute-start = (f32[64,8,128]{2,1,0:T(8,128)}, f32[64,8,128]{2,1,0:T(8,128)S(1)}, u32[]{:S(2)}, u32[]{:S(2)}) collective-permute-start(f32[64,8,128]{2,1,0:T(8,128)} %get-tuple-element.18), channel_id=1, source_target_pairs={{0,1},{1,2},{2,3},{3,4},{4,5},{5,6},{6,7},{7,8},{8,9},{9,10},{10,1... | collective-permute-start | bytes 786440 | tf_op jit(solution)/shard_map/ppermute | solution.py:332
  67.8 5.3 %collective-permute-start.1 = (f32[64,8,128]{2,1,0:T(8,128)}, f32[64,8,128]{2,1,0:T(8,128)S(1)}, u32[]{:S(2)}, u32[]{:S(2)}) collective-permute-start(f32[64,8,128]{2,1,0:T(8,128)} %get-tuple-element.19), channel_id=1, source_target_pairs={{1,0},{2,1},{3,2},{4,3},{5,4},{6,5},{7,6},{8,7},{9,8},{10,9},{11,1... | collective-permute-start | bytes 786440 | tf_op jit(solution)/shard_map/ppermute | solution.py:332
  69.2 4.0 %copy-start = (f32[64,8,128]{2,1,0:T(8,128)}, f32[64,8,128]{2,1,0:T(8,128)S(1)}, u32[]{:S(2)}) copy-start(f32[64,8,128]{2,1,0:T(8,128)S(1)} %collective-permute-done.refs_1_) | copy-start | bytes 786436
  73.2 0.7 copy-start.1
  97.5 8.0 %collective-permute-start.2 = (f32[8,128]{1,0:T(8,128)}, f32[8,128]{1,0:T(8,128)S(1)}, u32[]{:S(2)}, u32[]{:S(2)}) collective-permute-start(f32[8,128]{1,0:T(8,128)} %get-tuple-element.21), channel_id=1, source_target_pairs={{0,1},{1,2},{2,3},{3,4},{4,5},{5,6},{6,7},{7,8},{8,9},{9,10},{10,1... | collective-permute-start | bytes 12296 | tf_op jit(solution)/shard_map/ppermute | solution.py:332
  104.1 3.3 %collective-permute-start.3 = (f32[8,128]{1,0:T(8,128)}, f32[8,128]{1,0:T(8,128)S(1)}, u32[]{:S(2)}, u32[]{:S(2)}) collective-permute-start(f32[8,128]{1,0:T(8,128)} %get-tuple-element.22), channel_id=1, source_target_pairs={{1,0},{2,1},{3,2},{4,3},{5,4},{6,5},{7,6},{8,7},{9,8},{10,9},{11,1... | collective-permute-start | bytes 12296 | tf_op jit(solution)/shard_map/ppermute | solution.py:332
  105.5 2.0 %copy-start.2 = (f32[8,128]{1,0:T(8,128)}, f32[8,128]{1,0:T(8,128)S(1)}, u32[]{:S(2)}) copy-start(f32[8,128]{1,0:T(8,128)S(1)} %collective-permute-done.2.refs_1_) | copy-start | bytes 12292
  107.4 0.6 copy-start.4
  126.9 5.8 %collective-permute-start.4 = (f32[8,128]{1,0:T(8,128)}, f32[8,128]{1,0:T(8,128)S(1)}, u32[]{:S(2)}, u32[]{:S(2)}) collective-permute-start(f32[8,128]{1,0:T(8,128)} %get-tuple-element.27), channel_id=1, source_target_pairs={{0,1},{1,2},{2,3},{3,4},{4,5},{5,6},{6,7},{7,8},{8,9},{9,10},{10,1... | collective-permute-start | bytes 12296 | tf_op jit(solution)/shard_map/ppermute | solution.py:332
  131.4 3.3 %collective-permute-start.5 = (f32[8,128]{1,0:T(8,128)}, f32[8,128]{1,0:T(8,128)S(1)}, u32[]{:S(2)}, u32[]{:S(2)}) collective-permute-start(f32[8,128]{1,0:T(8,128)} %get-tuple-element.28), channel_id=1, source_target_pairs={{1,0},{2,1},{3,2},{4,3},{5,4},{6,5},{7,6},{8,7},{9,8},{10,9},{11,1... | collective-permute-start | bytes 12296 | tf_op jit(solution)/shard_map/ppermute | solution.py:332
  132.7 2.0 %copy-start.3 = (f32[8,128]{1,0:T(8,128)}, f32[8,128]{1,0:T(8,128)S(1)}, u32[]{:S(2)}) copy-start(f32[8,128]{1,0:T(8,128)S(1)} %collective-permute-done.4.refs_1_) | copy-start | bytes 12292
  134.7 0.6 copy-start.5
